TPU v7x, 128 devices: a whole 4x4x4 slice. The times are simulated.
128 devices in a mesh: band: 8 (over z, core), row: 16 (over x, y).
Axes of the slice: x: 4, y: 4, z: 4, core: 2. Of those that a mesh axis runs over, the one named last changes fastest.
Arguments:
- recorded: bfloat16 [1024, 1024, 512], P(('row', 'band')), may hold values from -5 to 5
- acquired: int32 [128, 128], replicated, may hold values 0 or 1
- partner: int32 [128], replicated, may hold values from 0 to 127, each once
- band_counts: int32 [8], replicated, may hold values from 1 to 6, 32 in all
- wavelet: float32 [2, 8], replicated, may hold values from -0.75 to 0.75, as said below
Outputs:
- primaries: bfloat16 [1024, 1024, 512], P(('row', 'band'))
Inputs may be any that keep to these rules, and one draw needn't show every extreme that they name: `partner`: a permutation of the 128 block indices. `band_counts`: the counts sum to 32; the largest is exactly 6. `wavelet`: each column, read as a complex number, has magnitude between 0.55 and 0.75.
All inputs are finite; a program needn't handle non-finite values.
Results may differ from a plain program's by a relative error of at most 0.0085.
Values may be sent and summed in bfloat16 or wider, within the bound.
No kernel may reach another device: no remote copies, remote signals or barrier semaphores. Data moves between devices by JAX's collectives and lax.ppermute only.
A program may use at most 128 MiB of HBM per device.

v0:
```python
import math

import jax
import jax.numpy as jnp
from jax import lax
from jax.sharding import PartitionSpec as P

NS = 1024
NT = 512
NF = 32
FLO = 4
BS = 8
ITERS = 5


def dft_tables():
    sample_index = jnp.arange(NT, dtype=jnp.int32)
    bin_index = FLO + jnp.arange(NF, dtype=jnp.int32)
    angles = (bin_index[:, None] * sample_index[None, :] % NT).astype(jnp.float32) * (
        2.0 * math.pi / NT
    )
    cycles = jnp.concatenate([jnp.cos(angles), -jnp.sin(angles)], axis=0)
    forward = (cycles * (1.0 / math.sqrt(NT))).astype(jnp.bfloat16)
    inverse = (cycles * math.sqrt(2.0 / NF)).astype(jnp.bfloat16)
    return (forward, inverse)


def shards(recorded, acquired, partner, band_counts, wavelet):
    band_size = lax.axis_size("band")
    row_size = lax.axis_size("row")
    band_index = lax.axis_index("band")
    row_index = lax.axis_index("row")
    shot_count = recorded.shape[0]
    stations = recorded.shape[1]
    devices = band_size * row_size
    first_shot = (row_index * band_size + band_index) * shot_count
    forward, inverse = dft_tables()
    offsets = jnp.arange(BS, dtype=jnp.int32)
    mirror_index = (BS * partner[:, None] + offsets[None, :]).reshape(stations)
    present = jnp.repeat(jnp.repeat(acquired, BS, axis=0), BS, axis=1) == 1
    own_present = lax.dynamic_slice_in_dim(present, first_shot, shot_count, 0)
    linear = jnp.arange(devices, dtype=jnp.int32)
    dest_block = linear % row_size * band_size + linear // row_size
    dest_shots = (
        dest_block[:, None] * shot_count + jnp.arange(shot_count, dtype=jnp.int32)[None, :]
    ).reshape(stations)
    send_order = jnp.take(mirror_index, dest_shots)
    source_device = mirror_index // shot_count
    source_place = (
        source_device % band_size * row_size + source_device // band_size
    ) * shot_count + mirror_index % shot_count
    outgoing = jnp.take(recorded, send_order, axis=1)
    incoming = lax.all_to_all(outgoing, ("band", "row"), split_axis=1, concat_axis=1, tiled=True)
    arranged = jnp.transpose(incoming.reshape(shot_count, devices, shot_count, NT), (2, 1, 0, 3))
    arranged = arranged.reshape(shot_count, stations, NT)
    mirrored = jnp.take(arranged, source_place, axis=1)
    traces = jnp.where(own_present[:, :, None], recorded, mirrored)
    spectra = jnp.einsum("ct,srt->csr", forward, traces, preferred_element_type=jnp.float32).astype(
        jnp.bfloat16
    )
    spectra = spectra.reshape(2, NF, shot_count, stations)
    band_ends = jnp.cumsum(band_counts)
    band_starts = band_ends - band_counts
    group_ids = jnp.arange(band_size, dtype=jnp.int32)
    slot_count = 3 * NF // (2 * band_size)
    slot_index = jnp.arange(slot_count, dtype=jnp.int32)
    chosen = jnp.minimum(band_starts[:, None] + slot_index[None, :], NF - 1).reshape(
        band_size * slot_count
    )
    outgoing = jnp.take(spectra, chosen, axis=1)
    local_rows = lax.all_to_all(outgoing, "band", split_axis=1, concat_axis=2, tiled=True)
    my_bins = lax.dynamic_slice_in_dim(chosen, band_index * slot_count, slot_count)
    my_group = jnp.sum((band_ends[None, :] <= my_bins[:, None]).astype(jnp.int32), axis=1)
    selector = (my_group[:, None] == group_ids[None, :]).astype(jnp.float32)
    rescale = 1.0 / math.sqrt(NS)
    wave_re = (jnp.sum(selector * wavelet[0][None, :], axis=1) * rescale)[:, None, None]
    wave_im = (jnp.sum(selector * wavelet[1][None, :], axis=1) * rescale)[:, None, None]
    whole_factor = lax.all_gather(local_rows, "row", axis=2, tiled=True)
    factor_re = (wave_re * whole_factor[0] - wave_im * whole_factor[1]).astype(jnp.bfloat16)
    factor_im = (wave_re * whole_factor[1] + wave_im * whole_factor[0]).astype(jnp.bfloat16)
    base_re = local_rows[0].astype(jnp.float32)
    base_im = local_rows[1].astype(jnp.float32)
    left_re = local_rows[0]
    left_im = local_rows[1]
    for sweep_turn in range(ITERS):
        real_part = jnp.einsum(
            "kra,kab->krb", left_re, factor_re, preferred_element_type=jnp.float32
        ) - jnp.einsum("kra,kab->krb", left_im, factor_im, preferred_element_type=jnp.float32)
        imag_part = jnp.einsum(
            "kra,kab->krb", left_re, factor_im, preferred_element_type=jnp.float32
        ) + jnp.einsum("kra,kab->krb", left_im, factor_re, preferred_element_type=jnp.float32)
        left_re = (base_re - real_part).astype(jnp.bfloat16)
        left_im = (base_im - imag_part).astype(jnp.bfloat16)
    result = jnp.stack([left_re, left_im], axis=0)
    returned = lax.all_to_all(result, "band", split_axis=2, concat_axis=1, tiled=True)
    bin_index = jnp.arange(NF, dtype=jnp.int32)
    bin_group = jnp.sum((band_ends[None, :] <= bin_index[:, None]).astype(jnp.int32), axis=1)
    bin_start = jnp.sum(
        jnp.where(bin_group[:, None] == group_ids[None, :], band_starts[None, :], 0), axis=1
    )
    slot_place = bin_group * slot_count + bin_index - bin_start
    returned = jnp.take(returned, slot_place, axis=1)
    merged = returned.reshape(2 * NF, shot_count, stations)
    output = jnp.einsum("csr,ct->srt", merged, inverse, preferred_element_type=jnp.float32)
    return output.astype(jnp.bfloat16)


def solution(mesh):
    return jax.shard_map(
        shards,
        mesh=mesh,
        in_specs=(P(("row", "band"), None, None), P(), P(), P(), P()),
        out_specs=P(("row", "band"), None, None),
        check_vma=False,
    )
```

profile of v0, /device:TPU:0, one launch (start us, length us, event | category | flops | bytes accessed | tf_op | source)
XLA Modules:
  0.0 565.1 jit_solution(17499981929077477578)
XLA Ops:
  12.3 35.6 %gather_fusion.3 = bf16[1024,8,512]{2,0,1:T(8,128)(2,1)} fusion(bf16[8,1024,512]{2,1,0:T(8,128)(2,1)} %param.7, s32[1024]{0:T(1024)S(1)} %broadcast_clamp_fusion.1), kind=kCustom, calls=%fused_computation.clone | custom fusion | bytes 16781312 | tf_op jit(solution)/shard_map/jit(_take)/gather | solution.py:52
  47.9 7.6 %select_bitcast_fusion = bf16[8,1024,512]{2,1,0:T(8,128)(2,1)} fusion(bf16[1024,8,512]{2,0,1:T(8,128)(2,1)} %gather_fusion.3, pred[1024]{0:T(1024)(128)(4,1)S(1)} %compare_and_fusion.1), kind=kLoop, calls=%fused_computation.19 | loop fusion | flops 4194304 | bytes 16778240 | tf_op jit(solution)/shard_map/jit(_take)/select_n | solution.py:52
  55.5 11.3 %copy.78 = bf16[8,1024,512]{2,0,1:T(8,128)(2,1)} copy(bf16[8,1024,512]{2,1,0:T(8,128)(2,1)} %select_bitcast_fusion) | data formatting | bytes 16777216 | tf_op jit(solution)/shard_map/jit(_take)/select_n | solution.py:52
  66.8 11.7 %all-to-all-start = ((bf16[8,1024,512]{2,0,1:T(8,128)(2,1)}), bf16[8,1024,512]{2,0,1:T(8,128)(2,1)}, u32[]{:S(2)}, u32[]{:S(2)}) async-start(bf16[8,1024,512]{2,0,1:T(8,128)(2,1)} %copy.78), calls=%async_computation | async-start | bytes 16777216 | tf_op jit(solution)/shard_map/all_to_all | solution.py:53
  81.1 95.5 %all-to-all-done = bf16[8,1024,512]{2,0,1:T(8,128)(2,1)} async-done(((bf16[8,1024,512]{2,0,1:T(8,128)(2,1)}), bf16[8,1024,512]{2,0,1:T(8,128)(2,1)}, u32[]{:S(2)}, u32[]{:S(2)}) %all-to-all-start) | async-done | bytes 8388640 | tf_op jit(solution)/shard_map/all_to_all | solution.py:53
  176.6 7.6 %copy.186 = bf16[8,128,8,512]{3,2,1,0:T(8,128)(2,1)} copy(bf16[8,128,8,512]{3,2,0,1:T(8,128)(2,1)} %bitcast.9) | data formatting | bytes 16777216 | tf_op jit(solution)/shard_map/transpose | solution.py:54
  184.2 11.3 %copy.81 = bf16[8,1024,512]{2,0,1:T(8,128)(2,1)} copy(bf16[8,1024,512]{2,1,0:T(8,128)(2,1)} %bitcast.171) | data formatting | bytes 16777216 | tf_op jit(solution)/shard_map/reshape | solution.py:55
  195.5 13.4 %gather_fusion.4 = bf16[1024,8,512]{2,1,0:T(8,128)(2,1)} fusion(bf16[8,1024,512]{2,0,1:T(8,128)(2,1)} %copy.81, s32[1024]{0:T(1024)S(1)} %broadcast_clamp_fusion), kind=kCustom, calls=%fused_computation.1.clone | custom fusion | bytes 16781312 | tf_op jit(solution)/shard_map/jit(_take)/gather | solution.py:56
  208.9 24.1 %bitcast_select_fusion = bf16[8,1024,512]{2,0,1:T(8,128)(2,1)S(1)} fusion(bf16[8,1024,512]{2,1,0:T(8,128)(2,1)} %param.7, bf16[1024,8,512]{2,1,0:T(8,128)(2,1)} %gather_fusion.4, pred[1024]{0:T(1024)(128)(4,1)S(1)} %get-tuple-element.8, pred[8,1024]{0,1:T(8,128)(4,1)S(1)} %constant_dynamic-slice_fusion), kind=kLoop, calls=%fused_computation.15 | loop fusion | flops 8388608 | bytes 25175040 | tf_op jit(solution)/shard_map/jit(_where)/select_n | solution.py:57
  233.0 4.9 fusion.48
  239.4 25.3 %all_to_all.41 = bf16[2,48,8,1024]{3,2,0,1:T(8,128)(2,1)S(1)} all-to-all(bf16[2,48,8,1024]{3,2,0,1:T(8,128)(2,1)S(1)} %select_bitcast_fusion.1), channel_id=1, replica_groups=mesh['band'=8,'row'=16] {'band'}, dimensions={1} | all-to-all | bytes 3145728 | tf_op jit(solution)/shard_map/all_to_all | solution.py:71
  267.1 154.0 %all-gather.2.cloned.1.call-done = bf16[2,6,1024,1024]{3,2,1,0:T(8,128)(2,1)} async-done(((bf16[2,6,64,1024]{3,2,1,0:T(8,128)(2,1)}), bf16[2,6,1024,1024]{3,2,1,0:T(8,128)(2,1)}) %all-gather.2.cloned.1.call-update) | async-done | bytes 25165840 | tf_op jit(solution)/shard_map/all_gather | solution.py:78
  421.2 13.2 %fusion.1 = (bf16[6,1024,1024]{2,1,0:T(8,128)(2,1)S(1)}, bf16[6,1024,1024]{2,1,0:T(8,128)(2,1)S(1)}) fusion(f32[6]{0:T(128)S(1)} %get-tuple-element.18, f32[6]{0:T(128)S(1)} %get-tuple-element.19, bf16[2,6,1024,1024]{3,2,1,0:T(8,128)(2,1)} %all-gather.2.cloned.1.call-done), kind=kLoop, calls=%fused_computation.10 | loop fusion | flops 62914560 | bytes 50331696 | tf_op jit(solution)/shard_map/convert_element_type | solution.py:79
  455.0 5.6 fusion.44
  460.6 5.3 fusion.46
  465.9 4.9 fusion.32
  470.9 4.9 fusion.34
  475.8 5.0 fusion.36
  488.7 5.9 %fusion.26 = f32[6,64,1024]{2,1,0:T(8,128)} fusion(bf16[6,1024,1024]{2,1,0:T(8,128)(2,1)S(1)} %get-tuple-element.11, f32[6,64,1024]{2,1,0:T(8,128)} %fusion.36, f32[6,64,1024]{2,1,0:T(8,128)S(1)} %copy-done.5, bf16[1,6,8,8,1024]{4,3,1,2,0:T(8,128)(2,1)S(1)} %get-tuple-element.12), kind=kOutput, calls=%fused_computation.51 | convolution fusion | flops 806879232 | bytes 18087936 | tf_op jit(solution)/shard_map/kra,kab->krb/dot_general | solution.py:88
  498.8 5.9 %fusion.30 = f32[6,64,1024]{2,1,0:T(8,128)} fusion(bf16[6,1024,1024]{2,1,0:T(8,128)(2,1)S(1)} %get-tuple-element.10, f32[6,64,1024]{2,1,0:T(8,128)} %fusion.38, f32[6,64,1024]{2,1,0:T(8,128)} %fusion.34, bf16[1,6,8,8,1024]{4,3,1,2,0:T(8,128)(2,1)S(1)} %get-tuple-element.13), kind=kOutput, calls=%fused_computation.53 | convolution fusion | flops 806879232 | bytes 18087936 | tf_op jit(solution)/shard_map/kra,kab->krb/dot_general | solution.py:86
  508.3 5.3 fusion.20
  513.6 4.8 fusion.58
  528.8 21.3 %all-to-all-done.2 = bf16[2,6,64,1024]{3,0,1,2:T(2,128)(2,1)S(1)} async-done(((bf16[2,6,64,1024]{3,0,1,2:T(2,128)(2,1)}), bf16[2,6,64,1024]{3,0,1,2:T(2,128)(2,1)S(1)}, u32[]{:S(2)}, u32[]{:S(2)}) %all-to-all-start.2) | async-done | bytes 1572896 | tf_op jit(solution)/shard_map/all_to_all | solution.py:95
  552.2 5.8 %convolution_convert_fusion = bf16[8,1024,512]{2,1,0:T(8,128)(2,1)} fusion(bf16[64,8,1024]{2,1,0:T(8,128)(2,1)S(1)} %bitcast_select_fusion.1, f32[32,512]{1,0:T(8,128)S(1)} %copy-done.11, f32[32,512]{1,0:T(8,128)S(1)} %copy-done.9), kind=kOutput, calls=%fused_computation.20 | convolution fusion | flops 541163520 | bytes 9568256 | tf_op jit(solution)/shard_map/csr,ct->srt/dot_general | solution.py:104
  (102 shorter events, 60.6 us)
Async XLA Ops:
  66.8 12.1 %copy-start.16 = (s32[8]{0:T(128)S(1)}, s32[8]{0:T(128)}, u32[]{:S(2)}) copy-start(s32[8]{0:T(128)} %param.10) | copy-start | bytes 100
  66.8 12.7 %copy-start.12 = (s32[128,128]{1,0:T(8,128)S(1)}, s32[128,128]{1,0:T(8,128)}, u32[]{:S(2)}) copy-start(s32[128,128]{1,0:T(8,128)} %param.8) | copy-start | bytes 196612
  66.8 109.8 %all-to-all-start = ((bf16[8,1024,512]{2,0,1:T(8,128)(2,1)}), bf16[8,1024,512]{2,0,1:T(8,128)(2,1)}, u32[]{:S(2)}, u32[]{:S(2)}) async-start(bf16[8,1024,512]{2,0,1:T(8,128)(2,1)} %copy.78), calls=%async_computation | async-start | bytes 16777216 | tf_op jit(solution)/shard_map/all_to_all | solution.py:53
  78.5 342.6 %all-gather.2.cloned.1.call-start = ((), (), s32[]{:S(2)}) async-start(), calls=%async_computation.3 | async-start | bytes 26738688 | tf_op jit(solution)/shard_map/all_gather | solution.py:78
  79.1 0.5 copy-start.14
  81.0 151.9 %copy-start.8 = (f32[32,512]{1,0:T(8,128)}, f32[32,512]{1,0:T(8,128)S(1)}, u32[]{:S(2)}) copy-start(f32[32,512]{1,0:T(8,128)S(1)} %get-tuple-element.16) | copy-start | bytes 196612
  81.0 151.9 %copy-start.10 = (f32[32,512]{1,0:T(8,128)}, f32[32,512]{1,0:T(8,128)S(1)}, u32[]{:S(2)}) copy-start(f32[32,512]{1,0:T(8,128)S(1)} %get-tuple-element.17) | copy-start | bytes 196612
  265.9 0.7 copy-start.13
  436.7 10.4 %copy-start.6 = (f32[6,64,1024]{2,1,0:T(8,128)}, f32[6,64,1024]{2,1,0:T(8,128)S(1)}, u32[]{:S(2)}) copy-start(f32[6,64,1024]{2,1,0:T(8,128)S(1)} %fusion.69) | copy-start | bytes 4718596
  475.8 5.1 copy-start.4
  484.4 4.3 copy-start.5
  488.7 16.0 %copy-start = (f32[6,64,1024]{2,1,0:T(8,128)}, f32[6,64,1024]{2,1,0:T(8,128)S(1)}, u32[]{:S(2)}) copy-start(f32[6,64,1024]{2,1,0:T(8,128)S(1)} %fusion.24) | copy-start | bytes 4718596
  498.8 5.9 %copy-start.2 = (f32[6,64,1024]{2,1,0:T(8,128)}, f32[6,64,1024]{2,1,0:T(8,128)S(1)}, u32[]{:S(2)}) copy-start(f32[6,64,1024]{2,1,0:T(8,128)S(1)} %fusion.28) | copy-start | bytes 4718596
  513.6 4.8 copy-start.1
  513.6 4.9 copy-start.3
  513.6 4.9 copy-start.7
  523.9 4.7 copy-start.15
  523.9 26.1 %all-to-all-start.2 = ((bf16[2,6,64,1024]{3,0,1,2:T(2,128)(2,1)}), bf16[2,6,64,1024]{3,0,1,2:T(2,128)(2,1)S(1)}, u32[]{:S(2)}, u32[]{:S(2)}) async-start(bf16[2,6,64,1024]{3,0,1,2:T(2,128)(2,1)} %copy.89), calls=%async_computation.2 | async-start | bytes 3145728 | tf_op jit(solution)/shard_map/all_to_all | solution.py:95
  551.4 0.8 copy-start.9
  551.4 0.9 copy-start.11
Sparse Core Ops, SparseCore 0:
  266.1 155.0 all-gather.1
where the time goes:
time: 574 us; the launch traced here: 565 us
  waiting for transfers between devices  271 us (47%)
  matrix products  96.9 us (17%)
  local copies, waits for them, and re-layouts  93.8 us (16%)
  other arithmetic  47.6 us (8%)
  blocking collectives  25.3 us (4%)
  starting transfers between devices  16.6 us (3%)
  between operations  14 us (2%)
    all_gather x1, waiting for transfers between devices, shards(): whole_factor = lax.all_gather(local_rows, 'row', axis=2, tiled=True)  154 us
    all_to_all x1, waiting for transfers between devices, shards(): lax.all_to_all(outgoing, ('band', 'row'), split_axis=1, concat_axis=1, ti...  95.5 us
    gather x1, local copies, waits for them, and re-layouts, shards(): outgoing = jnp.take(recorded, send_order, axis=1)  35.6 us
    all_to_all x1, blocking collectives, shards(): lax.all_to_all(outgoing, 'band', split_axis=1, concat_axis=2, tiled=True)  25.3 us
    select_n x1, other arithmetic, shards(): traces = jnp.where(own_present[:, :, None], recorded, mirrored)  24.1 us
    dot_general x5, matrix products, shards(): jnp.einsum('kra,kab->krb', left_re, factor_im, preferred_element_type=jnp...  23.5 us
    dot_general x5, matrix products, shards(): jnp.einsum('kra,kab->krb', left_re, factor_re, preferred_element_type=jnp...  23 us
    dot_general x5, matrix products, shards(): jnp.einsum('kra,kab->krb', left_im, factor_im, preferred_element_type=jnp...  22.1 us
  transfers between devices with their start and end apart: 3, of which 3 were waited for; matrix products, arithmetic and copies ran while one was open for 1% of the time, Pallas kernels for 0%

commit v1 on v0

v1 whole, which is shorter than its diff:
```python
import math

import jax
import jax.numpy as jnp
import ml_dtypes
import numpy as np
from jax import lax
from jax.experimental import pallas as pl
from jax.experimental.pallas import tpu as pltpu
from jax.sharding import Mesh
from jax.sharding import PartitionSpec as P

NS = 1024
NT = 512
NF = 32
FLO = 4
BS = 8
ITERS = 5
NB = NS // BS
GROUP = 32
OWN = GROUP * BS
ALL_AXES = ("z_hi", "z_lo", "core", "x", "y")
BIN_AXES = ("z_lo", "x", "y")
SHOT_AXES = ("x", "y", "z_hi", "z_lo", "core")


def dft_tables():
    sample_index = np.arange(NT, dtype=np.int32)
    bin_index = FLO + np.arange(NF, dtype=np.int32)
    angles = (bin_index[:, None] * sample_index[None, :] % NT).astype(np.float32) * np.float32(
        2.0 * math.pi / NT
    )
    cycles = np.concatenate([np.cos(angles), -np.sin(angles)], axis=0).astype(np.float32)
    forward = (cycles * np.float32(1.0 / math.sqrt(NT))).astype(ml_dtypes.bfloat16)
    inverse = (cycles * np.float32(math.sqrt(2.0 / NF))).astype(ml_dtypes.bfloat16)
    return (forward, inverse)


def source_of(block):
    return (block % 8) * 16 + block // 8


def solve_kernel(
    partner, place, wave, acquired, first, second, out, mirror, factor, left, base, mask
):
    parts = (first, second)
    column_block = lax.broadcasted_iota(jnp.int32, (NB, NS), 1) // BS
    expand = (column_block == lax.broadcasted_iota(jnp.int32, (NB, NS), 0)).astype(jnp.bfloat16)
    mask[...] = jnp.dot(
        acquired[...].astype(jnp.float32).astype(jnp.bfloat16),
        expand,
        preferred_element_type=jnp.float32,
    )

    def turn(group, carry):
        blocks = [partner[group * 16 + i] for i in range(16)]
        for part in range(2):
            rows = jnp.concatenate(
                [parts[part][source_of(block)].astype(jnp.float32) for block in blocks], axis=0
            )
            mirror[part, :, pl.ds(pl.multiple_of(group * 128, 128), 128)] = rows.T
        return carry

    lax.fori_loop(0, NB // 16, turn, 0)

    def filled(block):
        keep = mask[pl.ds(block, 1), :] > 0.5
        row = pl.multiple_of(partner[block] * BS, BS)
        source = source_of(block)
        return tuple(
            jnp.where(
                keep, parts[part][source].astype(jnp.float32), mirror[part, pl.ds(row, BS), :]
            )
            for part in range(2)
        )

    def scale(pair, carry):
        upper = filled(pair * 2)
        lower = filled(pair * 2 + 1)
        real = jnp.concatenate([upper[0], lower[0]], axis=0)
        imag = jnp.concatenate([upper[1], lower[1]], axis=0)
        row = pl.multiple_of(pair * 16, 16)
        factor[pl.ds(row, 16), :] = (wave[0] * real - wave[1] * imag).astype(jnp.bfloat16)
        factor[pl.ds(NS + row, 16), :] = (wave[0] * imag + wave[1] * real).astype(jnp.bfloat16)
        return carry

    lax.fori_loop(0, NB // 2, scale, 0)

    def put(slot, row, rows, real, imag, column, columns):
        real_low = real.astype(jnp.bfloat16)
        imag_low = imag.astype(jnp.bfloat16)
        left[slot, pl.ds(row, rows), pl.ds(column, columns)] = real_low
        left[slot, pl.ds(row, rows), pl.ds(NS + column, columns)] = -imag_low
        left[slot, pl.ds(OWN + row, rows), pl.ds(column, columns)] = imag_low
        left[slot, pl.ds(OWN + row, rows), pl.ds(NS + column, columns)] = real_low

    def own(pair, carry):
        blocks = []
        for i in range(2):
            member = pair * 2 + i
            blocks.append(filled((member % 16) * 8 + (member // 16) * 2 + place[0]))
        real = jnp.concatenate([blocks[0][0], blocks[1][0]], axis=0)
        imag = jnp.concatenate([blocks[0][1], blocks[1][1]], axis=0)
        row = pl.multiple_of(pair * 16, 16)
        base[pl.ds(row, 16), :] = real
        base[pl.ds(OWN + row, 16), :] = imag
        put(0, row, 16, real, imag, 0, NS)
        return carry

    lax.fori_loop(0, GROUP // 2, own, 0)

    width = 256

    def sweep(slot, last):
        for tile in range(NS // width):
            columns = pl.ds(tile * width, width)
            product = jnp.dot(
                left[slot], factor[:, columns], preferred_element_type=jnp.float32
            )
            value = base[:, columns] - product
            if last:
                out[:, 0, :, columns] = (
                    value[:OWN].reshape(GROUP, BS, width).astype(jnp.bfloat16)
                )
                out[:, 1, :, columns] = (
                    value[OWN:].reshape(GROUP, BS, width).astype(jnp.bfloat16)
                )
            else:
                put(1 - slot, 0, OWN, value[:OWN], value[OWN:], tile * width, width)

    for turn_index in range(ITERS):
        sweep(turn_index % 2, turn_index == ITERS - 1)


def solve(partner, place, wave, acquired, first, second):
    smem = pl.BlockSpec(memory_space=pltpu.SMEM)
    vmem = pl.BlockSpec(memory_space=pltpu.VMEM)
    return pl.pallas_call(
        solve_kernel,
        out_shape=jax.ShapeDtypeStruct((GROUP, 2, BS, NS), jnp.bfloat16),
        in_specs=[smem, smem, smem, vmem, vmem, vmem],
        out_specs=vmem,
        scratch_shapes=[
            pltpu.VMEM((2, NS, NS), jnp.float32),
            pltpu.VMEM((2 * NS, NS), jnp.bfloat16),
            pltpu.VMEM((2, 2 * OWN, 2 * NS), jnp.bfloat16),
            pltpu.VMEM((2 * OWN, NS), jnp.float32),
            pltpu.VMEM((NB, NS), jnp.float32),
        ],
        compiler_params=pltpu.CompilerParams(vmem_limit_bytes=48 * 1024 * 1024),
        name="solve",
    )(partner, place, wave, acquired, first, second)


def shards(recorded, acquired, partner, band_counts, wavelet):
    core = lax.axis_index("core")
    z_hi = lax.axis_index("z_hi")
    my_bin = lax.axis_index("z_lo") * 16 + lax.axis_index("x") * 4 + lax.axis_index("y")
    forward, inverse = dft_tables()
    ordered = np.tile(forward.reshape(2, 2, 16, NT).transpose(1, 0, 2, 3).reshape(64, NT), (2, 1))
    outgoing = jnp.einsum(
        "ct,srt->csr", jnp.asarray(ordered), recorded, preferred_element_type=jnp.float32
    ).astype(jnp.bfloat16)
    first = lax.all_to_all(outgoing, ALL_AXES, split_axis=0, concat_axis=0, tiled=True)
    second = lax.ppermute(first, "core", [(0, 1), (1, 0)])

    band_ends = jnp.cumsum(band_counts)
    my_group = jnp.sum((band_ends <= my_bin).astype(jnp.int32))
    chosen = (jnp.arange(8, dtype=jnp.int32) == my_group).astype(jnp.float32)
    rescale = 1.0 / math.sqrt(NS)
    wave = jnp.sum(wavelet * chosen[None, :], axis=1) * rescale
    wave = jnp.where(core == 0, wave, -wave[::-1])
    place = (z_hi * 4 + core).astype(jnp.int32).reshape(1)
    estimate = solve(partner, place, wave, acquired, first, second)

    returned = lax.all_to_all(estimate, BIN_AXES, split_axis=0, concat_axis=0, tiled=True)
    table = inverse.reshape(2, NF, NT)
    table = jnp.where(core == 0, jnp.asarray(table), jnp.asarray(table[::-1]))
    output = jnp.einsum("kcsr,ckt->srt", returned, table, preferred_element_type=jnp.float32)
    return output.astype(jnp.bfloat16)


def solution(mesh):
    fine = Mesh(mesh.devices.reshape(2, 2, 2, 4, 4), ALL_AXES)
    return jax.shard_map(
        shards,
        mesh=fine,
        in_specs=(P(SHOT_AXES, None, None), P(), P(), P(), P()),
        out_specs=P(SHOT_AXES, None, None),
        check_vma=False,
    )
```

time: 574 us -> 98.2 us (0.17); the launches traced: 565 us -> 98 us
  waiting for transfers between devices: 271 us -> 2.6 us
  local copies, waits for them, and re-layouts: 93.8 us -> 1.28 us
  matrix products: 96.9 us -> 12.1 us
  other arithmetic: 47.6 us -> 1.57 us
  blocking collectives: 25.3 us -> 61.7 us
  Pallas kernels: 0 us -> 18.7 us
  starting transfers between devices: 16.6 us -> 0.01 us
  between operations: 14 us -> 0.06 us
    all_gather x1 -> x0, waiting for transfers between devices: 154 us -> none  [shards(): whole_factor = lax.all_gather(local_rows, 'row', axis=2, tiled=True)]
    all_to_all x2 -> x0, waiting for transfers between devices: 117 us -> none  [the longest x1 95.5 us: shards(): lax.all_to_all(outgoing, ('band', 'row'), split_axis=1, concat_axis=1, ti...]
    dot_general x22 -> x2, matrix products: 96.9 us -> 12.1 us  [the longest x1 6.31 us: shards(): jnp.einsum('ct,srt->csr', jnp.asarray(ordered), recorded, preferred_eleme...]
    gather x6 -> x0, local copies, waits for them, and re-layouts: 54.9 us -> none  [the longest x1 35.6 us: shards(): outgoing = jnp.take(recorded, send_order, axis=1)]
    all_to_all x1 -> x2, blocking collectives: 25.3 us -> 61.7 us  [the longest x1 40.8 us: shards(): lax.all_to_all(outgoing, ALL_AXES, split_axis=0, concat_axis=0, tiled=True)]
    select_n x7 -> x1, other arithmetic: 32.1 us -> 0.01 us  [shards(): wave = jnp.where(core == 0, wave, -wave[::-1])]
    pallas_call x0 -> x1, Pallas kernels: none -> 18.7 us  [solve(): pl.pallas_call(solve_kernel, out_shape=jax.ShapeDtypeStruct((GROUP, 2, BS...]
    all_to_all x2 -> x0, starting transfers between devices: 16.3 us -> none  [the longest x1 11.7 us: shards(): lax.all_to_all(outgoing, ('band', 'row'), split_axis=1, concat_axis=1, ti...]
  transfers between devices with their start and end apart: 3 -> 1, of which waited for: 3 -> 1; matrix products, arithmetic and copies ran while one was open for 1% -> 2% of each run, Pallas kernels for 0% -> 0%
where the time goes in v1:
time: 98.2 us; the launch traced here: 98 us
  blocking collectives  61.7 us (63%)
  Pallas kernels  18.7 us (19%)
  matrix products  12.1 us (12%)
  waiting for transfers between devices  2.6 us (3%)
  other arithmetic  1.57 us (2%)
  local copies, waits for them, and re-layouts  1.28 us (1%)
    all_to_all x1, blocking collectives, shards(): lax.all_to_all(outgoing, ALL_AXES, split_axis=0, concat_axis=0, tiled=True)  40.8 us
    all_to_all x1, blocking collectives, shards(): lax.all_to_all(estimate, BIN_AXES, split_axis=0, concat_axis=0, tiled=True)  20.9 us
    pallas_call x1, Pallas kernels, solve(): pl.pallas_call(solve_kernel, out_shape=jax.ShapeDtypeStruct((GROUP, 2, BS...  18.7 us
    dot_general x1, matrix products, shards(): jnp.einsum('ct,srt->csr', jnp.asarray(ordered), recorded, preferred_eleme...  6.31 us
    dot_general x1, matrix products, shards(): jnp.einsum('kcsr,ckt->srt', returned, table, preferred_element_type=jnp.f...  5.8 us
    ppermute x1, waiting for transfers between devices, shards(): second = lax.ppermute(first, 'core', [(0, 1), (1, 0)])  2.6 us
  transfers between devices with their start and end apart: 1, of which 1 were waited for; matrix products, arithmetic and copies ran while one was open for 2% of the time, Pallas kernels for 0%

profile of v1, /device:TPU:0, one launch (start us, length us, event | category | flops | bytes accessed | tf_op | source)
XLA Modules:
  0.0 98.0 jit_solution(5771896856843531874)
XLA Ops:
  0.0 0.0 copy-start.4
  0.0 0.0 copy-start.1
  0.0 0.0 copy-start
  0.0 6.3 %fusion.5 = bf16[128,8,1024]{2,0,1:T(8,128)(2,1)S(1)} fusion(bf16[128,512,1]{1,0,2:T(8,128)(2,1)} %constant.44, bf16[8,1024,512]{2,1,0:T(8,128)(2,1)} %param.8), kind=kOutput, calls=%fused_computation.11 | convolution fusion | flops 1073741824 | bytes 10616832 | tf_op jit(solution)/shard_map/ct,srt->csr/dot_general | solution.py:161
  6.3 0.0 copy-start.2
  6.3 0.0 copy-start.3
  6.3 1.2 %copy.15 = bf16[128,8,1024]{2,1,0:T(8,128)(2,1)S(1)} copy(bf16[128,8,1024]{2,0,1:T(8,128)(2,1)S(1)} %fusion.5) | data formatting | bytes 4194304 | tf_op jit(solution)/shard_map/ct,srt->csr/dot_general | solution.py:161
  7.5 40.8 %all_to_all.10.first = bf16[128,8,1024]{2,1,0:T(8,128)(2,1)S(1)} all-to-all(bf16[128,8,1024]{2,1,0:T(8,128)(2,1)S(1)} %copy.15), channel_id=1, replica_groups=mesh['z_hi'=2,'z_lo'=2,'core'=2,'x'=4,'y'=4] {'z_hi','z_lo','core','x','y'}, dimensions={0} | all-to-all | bytes 4194304 | tf_op jit(solution)/shard_map/all_to_all | solution.py:164
  48.3 0.0 collective-permute-start
  48.3 0.0 copy-done.5
  48.3 0.2 reduce-window.9
  48.5 0.6 fusion.4
  49.1 0.6 compare_convert_fusion
  49.7 0.0 copy-done.4
  49.8 0.1 multiply_reduce_fusion
  49.9 0.1 reverse.3
  50.0 2.6 %collective-permute-done.second = bf16[128,8,1024]{2,1,0:T(8,128)(2,1)} collective-permute-done((bf16[128,8,1024]{2,1,0:T(8,128)(2,1)S(1)}, bf16[128,8,1024]{2,1,0:T(8,128)(2,1)}, u32[]{:S(2)}, u32[]{:S(2)}) %collective-permute-start) | collective-permute-done | bytes 2097184 | tf_op jit(solution)/shard_map/ppermute | solution.py:165
  52.6 0.0 copy-done.1
  52.6 0.0 copy-done
  52.6 18.7 %solve.1 = bf16[32,2,8,1024]{3,2,1,0:T(8,128)(2,1)S(1)} custom-call(s32[128]{0:T(128)S(1)} %copy-done.1, s32[1]{0:T(128)} %bitcast.place, f32[2]{0:T(128)S(1)} %broadcast_select_fusion.wave, s32[128,128]{1,0:T(8,128)S(1)} %copy-done, bf16[128,8,1024]{2,1,0:T(8,128)(2,1)S(1)} %all_to_all.10.first, bf16[128,8,1024]{2,1,0:T(8,128)(2,1)} %collective-permute-done.second), custom_call_target="tpu_custom_call" | custom-call | tf_op jit(solution)/shard_map/solve/pallas_call | solution.py:138
  71.3 20.9 %all_to_all.11 = bf16[32,2,8,1024]{3,2,1,0:T(8,128)(2,1)S(1)} all-to-all(bf16[32,2,8,1024]{3,2,1,0:T(8,128)(2,1)S(1)} %solve.1), channel_id=1, replica_groups=mesh['z_hi'=2,'z_lo'=2,'core'=2,'x'=4,'y'=4] {'z_lo','x','y'}, dimensions={0} | all-to-all | bytes 2097152 | tf_op jit(solution)/shard_map/all_to_all | solution.py:176
  92.2 0.0 copy-done.2
  92.2 0.0 copy-done.3
  92.2 5.8 %bitcast_convert_fusion = bf16[8,1024,512]{2,1,0:T(8,128)(2,1)} fusion(bf16[32,2,8,1024]{3,2,1,0:T(8,128)(2,1)S(1)} %all_to_all.11, bf16[2,32,512]{2,1,0:T(8,128)(2,1)S(1)} %copy-done.3, bf16[2,32,512]{2,1,0:T(8,128)(2,1)S(1)} %copy-done.2, pred[]{:T(512)S(6)} %eq.14), kind=kOutput, calls=%fused_computation | convolution fusion | flops 541097984 | bytes 9568257 | tf_op jit(solution)/shard_map/kcsr,ckt->srt/dot_general | solution.py:179
  (2 shorter events, 0.0 us)
Async XLA Ops:
  0.0 48.3 %copy-start.5 = (s32[8]{0:T(128)S(1)}, s32[8]{0:T(128)}, u32[]{:S(2)}) copy-start(s32[8]{0:T(128)} %param.11) | copy-start | bytes 100
  0.0 49.7 %copy-start.4 = (f32[2,8]{1,0:T(2,128)S(1)}, f32[2,8]{1,0:T(2,128)}, u32[]{:S(2)}) copy-start(f32[2,8]{1,0:T(2,128)} %param.12) | copy-start | bytes 196
  0.0 52.6 %copy-start.1 = (s32[128]{0:T(128)S(1)}, s32[128]{0:T(128)}, u32[]{:S(2)}) copy-start(s32[128]{0:T(128)} %partner.1) | copy-start | bytes 1540
  0.0 52.6 %copy-start = (s32[128,128]{1,0:T(8,128)S(1)}, s32[128,128]{1,0:T(8,128)}, u32[]{:S(2)}) copy-start(s32[128,128]{1,0:T(8,128)} %acquired.1) | copy-start | bytes 196612
  6.3 85.9 %copy-start.2 = (bf16[2,32,512]{2,1,0:T(8,128)(2,1)S(1)}, bf16[2,32,512]{2,1,0:T(8,128)(2,1)}, u32[]{:S(2)}) copy-start(bf16[2,32,512]{2,1,0:T(8,128)(2,1)} %constant.42.clone) | copy-start | bytes 196612
  6.3 85.9 %copy-start.3 = (bf16[2,32,512]{2,1,0:T(8,128)(2,1)S(1)}, bf16[2,32,512]{2,1,0:T(8,128)(2,1)}, u32[]{:S(2)}) copy-start(bf16[2,32,512]{2,1,0:T(8,128)(2,1)} %constant.41.clone) | copy-start | bytes 196612
  48.3 4.3 %collective-permute-start = (bf16[128,8,1024]{2,1,0:T(8,128)(2,1)S(1)}, bf16[128,8,1024]{2,1,0:T(8,128)(2,1)}, u32[]{:S(2)}, u32[]{:S(2)}) collective-permute-start(bf16[128,8,1024]{2,1,0:T(8,128)(2,1)S(1)} %all_to_all.10.first), channel_id=1, source_target_pairs={{0,16},{16,0},{1,17},{17,1},{2,18},{18,2},{3,19},{19,3},{4,20},{20... | collective-permute-start | bytes 6291464 | tf_op jit(solution)/shard_map/ppermute | solution.py:165

commit v2 on v1

v2 whole, which is shorter than its diff:
```python
import math

import jax
import jax.numpy as jnp
import ml_dtypes
import numpy as np
from jax import lax
from jax.experimental import pallas as pl
from jax.experimental.pallas import tpu as pltpu
from jax.sharding import Mesh
from jax.sharding import PartitionSpec as P

NS = 1024
NT = 512
NF = 32
FLO = 4
BS = 8
ITERS = 5
NB = NS // BS
GROUP = 32
OWN = GROUP * BS
ALL_AXES = ("z_hi", "z_lo", "core", "x", "y")
BIN_AXES = ("z_lo", "x", "y")
SHOT_AXES = ("x", "y", "z_hi", "z_lo", "core")


def dft_tables():
    sample_index = np.arange(NT, dtype=np.int32)
    bin_index = FLO + np.arange(NF, dtype=np.int32)
    angles = (bin_index[:, None] * sample_index[None, :] % NT).astype(np.float32) * np.float32(
        2.0 * math.pi / NT
    )
    cycles = np.concatenate([np.cos(angles), -np.sin(angles)], axis=0).astype(np.float32)
    forward = (cycles * np.float32(1.0 / math.sqrt(NT))).astype(ml_dtypes.bfloat16)
    inverse = (cycles * np.float32(math.sqrt(2.0 / NF))).astype(ml_dtypes.bfloat16)
    return (forward, inverse)


def source_of(block):
    return (block % 8) * 16 + block // 8


def transform_kernel(table_from, traces, out, table, held, wide, sems):
    shots = traces.shape[0]
    copies = [pltpu.make_async_copy(traces.at[s], held.at[s], sems.at[s]) for s in range(shots)]
    table_copy = pltpu.make_async_copy(table_from, table, sems.at[shots])
    table_copy.start()
    for copy in copies:
        copy.start()
    table_copy.wait()
    for s in range(shots):
        copies[s].wait()
        wide[s] = lax.dot_general(
            table[...], held[s], (((1,), (1,)), ((), ())), preferred_element_type=jnp.float32
        )
    ordered = jnp.transpose(wide[...], (1, 0, 2)).astype(jnp.bfloat16)
    out[:64] = ordered
    out[64:] = ordered


def transform(table, traces):
    vmem = pl.BlockSpec(memory_space=pltpu.VMEM)
    return pl.pallas_call(
        transform_kernel,
        out_shape=jax.ShapeDtypeStruct((NB, BS, NS), jnp.bfloat16),
        in_specs=[pl.BlockSpec(memory_space=pltpu.HBM)] * 2,
        out_specs=vmem,
        scratch_shapes=[
            pltpu.VMEM((2 * NF, NT), jnp.bfloat16),
            pltpu.VMEM((BS, NS, NT), jnp.bfloat16),
            pltpu.VMEM((BS, 2 * NF, NS), jnp.float32),
            pltpu.SemaphoreType.DMA((BS + 1,)),
        ],
        compiler_params=pltpu.CompilerParams(vmem_limit_bytes=24 * 1024 * 1024),
        name="transform",
    )(table, traces)


def restore_kernel(place, spectra, tables, out, wide, held, sems):
    wide[...] = jnp.transpose(
        spectra[...].astype(jnp.float32).reshape(2 * NF, BS, NS), (1, 0, 2)
    )
    table = tables[place[1]]
    copies = []
    for s in range(BS):
        held[s] = lax.dot_general(
            wide[s].astype(jnp.bfloat16),
            table,
            (((0,), (0,)), ((), ())),
            preferred_element_type=jnp.float32,
        ).astype(jnp.bfloat16)
        copies.append(pltpu.make_async_copy(held.at[s], out.at[s], sems.at[s]))
        copies[-1].start()
    for copy in copies:
        copy.wait()


def restore(place, spectra, tables):
    vmem = pl.BlockSpec(memory_space=pltpu.VMEM)
    return pl.pallas_call(
        restore_kernel,
        out_shape=jax.ShapeDtypeStruct((BS, NS, NT), jnp.bfloat16),
        in_specs=[pl.BlockSpec(memory_space=pltpu.SMEM), vmem, vmem],
        out_specs=pl.BlockSpec(memory_space=pltpu.HBM),
        scratch_shapes=[
            pltpu.VMEM((BS, 2 * NF, NS), jnp.float32),
            pltpu.VMEM((BS, NS, NT), jnp.bfloat16),
            pltpu.SemaphoreType.DMA((BS,)),
        ],
        compiler_params=pltpu.CompilerParams(vmem_limit_bytes=24 * 1024 * 1024),
        name="restore",
    )(place, spectra, tables)


def fill(partner, acquired, rows, mirror, mask, filled):
    column_block = lax.broadcasted_iota(jnp.int32, (NB, NS), 1) // BS
    expand = (column_block == lax.broadcasted_iota(jnp.int32, (NB, NS), 0)).astype(jnp.bfloat16)
    mask[...] = jnp.dot(
        acquired[...].astype(jnp.float32).astype(jnp.bfloat16),
        expand,
        preferred_element_type=jnp.float32,
    )
    size = 256
    identity = (
        lax.broadcasted_iota(jnp.int32, (size, size), 0)
        == lax.broadcasted_iota(jnp.int32, (size, size), 1)
    ).astype(jnp.bfloat16)
    for group in range(NS // size):
        taken = jnp.concatenate(
            [
                rows[source_of(partner[group * (size // BS) + i])].astype(jnp.float32)
                for i in range(size // BS)
            ],
            axis=0,
        ).astype(jnp.bfloat16)
        for tile in range(NS // size):
            turned = lax.dot_general(
                identity,
                taken[:, tile * size : (tile + 1) * size],
                (((1,), (1,)), ((), ())),
                preferred_element_type=jnp.float32,
            )
            mirror[
                tile * (size // BS) : (tile + 1) * (size // BS),
                :,
                group * size : (group + 1) * size,
            ] = turned.reshape(size // BS, BS, size).astype(jnp.bfloat16)

    def choose(pair, carry):
        blocks = []
        for i in range(2):
            block = pair * 2 + i
            keep = mask[pl.ds(block, 1), :] > 0.5
            blocks.append(
                jnp.where(
                    keep,
                    rows[source_of(block)].astype(jnp.float32),
                    mirror[partner[block]].astype(jnp.float32),
                )
            )
        row = pl.multiple_of(pair * 16, 16)
        filled[pl.ds(row, 16), :] = jnp.concatenate(blocks, axis=0).astype(jnp.bfloat16)
        return carry

    lax.fori_loop(0, NB // 2, choose, 0, unroll=8)


def fill_first_kernel(partner, acquired, rows, filled, mirror, mask):
    fill(partner, acquired, rows, mirror, mask, filled)


def fill_first(partner, acquired, rows):
    vmem = pl.BlockSpec(memory_space=pltpu.VMEM)
    return pl.pallas_call(
        fill_first_kernel,
        out_shape=jax.ShapeDtypeStruct((NS, NS), jnp.bfloat16),
        in_specs=[pl.BlockSpec(memory_space=pltpu.SMEM), vmem, vmem],
        out_specs=vmem,
        scratch_shapes=[
            pltpu.VMEM((NB, BS, NS), jnp.bfloat16),
            pltpu.VMEM((NB, NS), jnp.float32),
        ],
        compiler_params=pltpu.CompilerParams(vmem_limit_bytes=16 * 1024 * 1024),
        name="fill_first",
    )(partner, acquired, rows)


def solve_kernel(
    partner, place, wave, acquired, first, rows, out, mirror, second, factor, left, base, mask
):
    fill(partner, acquired, rows, mirror, mask, second)

    def scale(pair, carry):
        row = pl.multiple_of(pair * 16, 16)
        real = first[pl.ds(row, 16), :].astype(jnp.float32)
        imag = second[pl.ds(row, 16), :].astype(jnp.float32)
        factor[pl.ds(row, 16), :] = (wave[0] * real - wave[1] * imag).astype(jnp.bfloat16)
        factor[pl.ds(NS + row, 16), :] = (wave[0] * imag + wave[1] * real).astype(jnp.bfloat16)
        return carry

    lax.fori_loop(0, NB // 2, scale, 0, unroll=8)

    def put(slot, row, rows, real, imag, column, columns):
        real_low = real.astype(jnp.bfloat16)
        imag_low = imag.astype(jnp.bfloat16)
        left[slot, pl.ds(row, rows), pl.ds(column, columns)] = real_low
        left[slot, pl.ds(row, rows), pl.ds(NS + column, columns)] = -imag_low
        left[slot, pl.ds(OWN + row, rows), pl.ds(column, columns)] = imag_low
        left[slot, pl.ds(OWN + row, rows), pl.ds(NS + column, columns)] = real_low

    def own(pair, carry):
        values = []
        for part in (first, second):
            blocks = []
            for i in range(2):
                member = pair * 2 + i
                chip = (member % 16) * 4 + member // 16 + place[0]
                both = part[pl.ds(pl.multiple_of(chip * 16, 16), 16), :].astype(jnp.float32)
                blocks.append(jnp.where(place[1] == 0, both[:BS], both[BS:]))
            values.append(jnp.concatenate(blocks, axis=0))
        row = pl.multiple_of(pair * 16, 16)
        base[pl.ds(row, 16), :] = values[0]
        base[pl.ds(OWN + row, 16), :] = values[1]
        put(0, row, 16, values[0], values[1], 0, NS)
        return carry

    lax.fori_loop(0, GROUP // 2, own, 0, unroll=4)

    width = 256

    def sweep(slot, last):
        for tile in range(NS // width):
            columns = pl.ds(tile * width, width)
            product = jnp.dot(
                left[slot], factor[:, columns], preferred_element_type=jnp.float32
            )
            value = base[:, columns] - product
            if last:
                out[:, 0, :, columns] = (
                    value[:OWN].reshape(GROUP, BS, width).astype(jnp.bfloat16)
                )
                out[:, 1, :, columns] = (
                    value[OWN:].reshape(GROUP, BS, width).astype(jnp.bfloat16)
                )
            else:
                put(1 - slot, 0, OWN, value[:OWN], value[OWN:], tile * width, width)

    for turn_index in range(ITERS):
        sweep(turn_index % 2, turn_index == ITERS - 1)


def solve(partner, place, wave, acquired, first, rows):
    smem = pl.BlockSpec(memory_space=pltpu.SMEM)
    vmem = pl.BlockSpec(memory_space=pltpu.VMEM)
    return pl.pallas_call(
        solve_kernel,
        out_shape=jax.ShapeDtypeStruct((GROUP, 2, BS, NS), jnp.bfloat16),
        in_specs=[smem, smem, smem, vmem, vmem, vmem],
        out_specs=vmem,
        scratch_shapes=[
            pltpu.VMEM((NB, BS, NS), jnp.bfloat16),
            pltpu.VMEM((NS, NS), jnp.bfloat16),
            pltpu.VMEM((2 * NS, NS), jnp.bfloat16),
            pltpu.VMEM((2, 2 * OWN, 2 * NS), jnp.bfloat16),
            pltpu.VMEM((2 * OWN, NS), jnp.float32),
            pltpu.VMEM((NB, NS), jnp.float32),
        ],
        compiler_params=pltpu.CompilerParams(vmem_limit_bytes=32 * 1024 * 1024),
        name="solve",
    )(partner, place, wave, acquired, first, rows)


def shards(recorded, acquired, partner, band_counts, wavelet):
    core = lax.axis_index("core")
    z_hi = lax.axis_index("z_hi")
    my_bin = lax.axis_index("z_lo") * 16 + lax.axis_index("x") * 4 + lax.axis_index("y")
    place = jnp.stack([z_hi * 2, core]).astype(jnp.int32)
    forward, inverse = dft_tables()
    ordered = forward.reshape(2, 2, 16, NT).transpose(1, 0, 2, 3).reshape(2 * NF, NT)
    outgoing = transform(jnp.asarray(ordered), recorded)
    first = lax.all_to_all(outgoing, ALL_AXES, split_axis=0, concat_axis=0, tiled=True)
    second = lax.ppermute(first, "core", [(0, 1), (1, 0)])
    filled = fill_first(partner, acquired, first)

    band_ends = jnp.cumsum(band_counts)
    my_group = jnp.sum((band_ends <= my_bin).astype(jnp.int32))
    chosen = (jnp.arange(8, dtype=jnp.int32) == my_group).astype(jnp.float32)
    rescale = 1.0 / math.sqrt(NS)
    wave = jnp.sum(wavelet * chosen[None, :], axis=1) * rescale
    wave = jnp.where(core == 0, wave, -wave[::-1])
    estimate = solve(partner, place, wave, acquired, filled, second)

    returned = lax.all_to_all(estimate, BIN_AXES, split_axis=0, concat_axis=0, tiled=True)
    paired = inverse.reshape(2, NF, NT).transpose(1, 0, 2)
    tables = np.stack([paired.reshape(2 * NF, NT), paired[:, ::-1].reshape(2 * NF, NT)])
    return restore(place, returned, jnp.asarray(tables))


def solution(mesh):
    fine = Mesh(mesh.devices.reshape(2, 2, 2, 4, 4), ALL_AXES)
    return jax.shard_map(
        shards,
        mesh=fine,
        in_specs=(P(SHOT_AXES, None, None), P(), P(), P(), P()),
        out_specs=P(SHOT_AXES, None, None),
        check_vma=False,
    )
```

time: 98.2 us -> 98.3 us (level)
  matrix products: 12.1 us -> 0 us
  Pallas kernels: 18.7 us -> 29.4 us
  local copies, waits for them, and re-layouts: 1.28 us -> 4.35 us
  waiting for transfers between devices: 2.6 us -> 0.01 us
    dot_general x2 -> x0, matrix products: 12.1 us -> none  [the longest x1 6.31 us: shards(): jnp.einsum('ct,srt->csr', jnp.asarray(ordered), recorded, preferred_eleme...]
    pallas_call x0 -> x3, Pallas kernels: none -> 12.1 us  [the longest x1 4.51 us: transform(): pl.pallas_call(transform_kernel, out_shape=jax.ShapeDtypeStruct((NB, BS,...]
    unnamed x12 -> x14, local copies, waits for them, and re-layouts: 0.03 us -> 4.25 us
    ppermute x1, waiting for transfers between devices: 2.6 us -> 0.01 us  [shards(): second = lax.ppermute(first, 'core', [(0, 1), (1, 0)])]
    pallas_call x1, Pallas kernels: 18.7 us -> 17.3 us  [solve(): pl.pallas_call(solve_kernel, out_shape=jax.ShapeDtypeStruct((GROUP, 2, BS...]
    dot_general x1 -> x0, local copies, waits for them, and re-layouts: 1.15 us -> none  [shards(): jnp.einsum('ct,srt->csr', jnp.asarray(ordered), recorded, preferred_eleme...]
  transfers between devices with their start and end apart: 1 -> 1, of which waited for: 1 -> 0; matrix products, arithmetic and copies ran while one was open for 2% -> 2% of each run, Pallas kernels for 0% -> 3%
where the time goes in v2:
time: 98.3 us; the launch traced here: 97.9 us
  blocking collectives  62.2 us (63%)
  Pallas kernels  29.4 us (30%)
  local copies, waits for them, and re-layouts  4.35 us (4%)
  other arithmetic  1.64 us (2%)
    all_to_all x1, blocking collectives, shards(): lax.all_to_all(outgoing, ALL_AXES, split_axis=0, concat_axis=0, tiled=True)  40.8 us
    all_to_all x1, blocking collectives, shards(): lax.all_to_all(estimate, BIN_AXES, split_axis=0, concat_axis=0, tiled=True)  21.5 us
    pallas_call x1, Pallas kernels, solve(): pl.pallas_call(solve_kernel, out_shape=jax.ShapeDtypeStruct((GROUP, 2, BS...  17.3 us
    pallas_call x1, Pallas kernels, transform(): pl.pallas_call(transform_kernel, out_shape=jax.ShapeDtypeStruct((NB, BS,...  4.51 us
    pallas_call x1, Pallas kernels, restore(): pl.pallas_call(restore_kernel, out_shape=jax.ShapeDtypeStruct((BS, NS, NT...  4.43 us
    unnamed x14, local copies, waits for them, and re-layouts  4.25 us
    pallas_call x1, Pallas kernels, fill_first(): pl.pallas_call(fill_first_kernel, out_shape=jax.ShapeDtypeStruct((NS, NS)...  3.14 us
  transfers between devices with their start and end apart: 1, of which 0 were waited for; matrix products, arithmetic and copies ran while one was open for 2% of the time, Pallas kernels for 3%

profile of v2, /device:TPU:0, one launch (start us, length us, event | category | flops | bytes accessed | tf_op | source)
XLA Modules:
  0.0 97.9 jit_solution(14067841735673378640)
XLA Ops:
  0.0 3.4 %copy-done = bf16[8,1024,512]{2,1,0:T(8,128)(2,1)S(1)} copy-done((bf16[8,1024,512]{2,1,0:T(8,128)(2,1)S(1)}, bf16[8,1024,512]{2,1,0:T(8,128)(2,1)}, u32[]{:S(2)}) %copy-start) | copy-done | bytes 8388632
  3.4 0.8 copy-done.3
  4.2 4.5 %transform.1 = bf16[128,8,1024]{2,1,0:T(8,128)(2,1)S(1)} custom-call(bf16[64,512]{1,0:T(8,128)(2,1)S(1)} %copy-done.3, bf16[8,1024,512]{2,1,0:T(8,128)(2,1)S(1)} %copy-done), custom_call_target="tpu_custom_call" | custom-call | tf_op jit(solution)/shard_map/transform/pallas_call | solution.py:63
  8.7 0.0 copy-start.6
  8.8 0.0 copy-start.5
  8.8 0.0 copy-start.1
  8.8 0.0 copy-start.4
  8.8 40.8 %all_to_all.10.rows = bf16[128,8,1024]{2,1,0:T(8,128)(2,1)S(1)} all-to-all(bf16[128,8,1024]{2,1,0:T(8,128)(2,1)S(1)} %transform.1), channel_id=1, replica_groups=mesh['z_hi'=2,'z_lo'=2,'core'=2,'x'=4,'y'=4] {'z_hi','z_lo','core','x','y'}, dimensions={0} | all-to-all | bytes 4194304 | tf_op jit(solution)/shard_map/all_to_all | solution.py:281
  49.5 0.0 collective-permute-start
  49.5 0.0 copy-done.6
  49.6 0.2 reduce-window.9
  49.7 0.6 fusion
  50.4 0.6 compare_convert_fusion
  51.0 0.0 copy-done.5
  51.0 0.1 multiply_reduce_fusion
  51.1 0.1 reverse.3
  51.2 0.1 pad_add_fusion.place
  51.3 0.0 copy-done.1
  51.3 3.1 %fill_first.1.first = bf16[1024,1024]{1,0:T(8,128)(2,1)S(1)} custom-call(s32[128]{0:T(128)S(1)} %copy-done.4, s32[128,128]{1,0:T(8,128)S(1)} %copy-done.1, bf16[128,8,1024]{2,1,0:T(8,128)(2,1)S(1)} %all_to_all.10.rows), custom_call_target="tpu_custom_call" | custom-call | tf_op jit(solution)/shard_map/fill_first/pallas_call | solution.py:174
  54.5 0.0 collective-permute-done.rows
  54.5 17.3 %solve.1 = bf16[32,2,8,1024]{3,2,1,0:T(8,128)(2,1)S(1)} custom-call(s32[128]{0:T(128)S(1)} %copy-done.4, s32[2]{0:T(128)S(1)} %pad_add_fusion.place, f32[2]{0:T(128)S(1)} %broadcast_select_fusion.wave, s32[128,128]{1,0:T(8,128)S(1)} %copy-done.1, bf16[1024,1024]{1,0:T(8,128)(2,1)S(1)} %fill_first.1.first, bf16[128,8,1024]{2,1,0:T(8,128)(2,1)} %collective-permute-done.rows), custom_call_target="tpu_custom_call" | custom-call | tf_op jit(solution)/shard_map/solve/pallas_call | solution.py:255
  71.8 0.0 copy-start.2
  71.8 21.5 %all_to_all.11.spectra = bf16[32,2,8,1024]{3,2,1,0:T(8,128)(2,1)S(1)} all-to-all(bf16[32,2,8,1024]{3,2,1,0:T(8,128)(2,1)S(1)} %solve.1), channel_id=1, replica_groups=mesh['z_hi'=2,'z_lo'=2,'core'=2,'x'=4,'y'=4] {'z_lo','x','y'}, dimensions={0} | all-to-all | bytes 2097152 | tf_op jit(solution)/shard_map/all_to_all | solution.py:293
  93.3 4.4 %restore.1 = bf16[8,1024,512]{2,1,0:T(8,128)(2,1)} custom-call(s32[2]{0:T(128)S(1)} %pad_add_fusion.place, bf16[32,2,8,1024]{3,2,1,0:T(8,128)(2,1)S(1)} %all_to_all.11.spectra, bf16[2,64,512]{2,1,0:T(8,128)(2,1)S(1)} %copy-done.2), custom_call_target="tpu_custom_call" | custom-call | tf_op jit(solution)/shard_map/restore/pallas_call | solution.py:100
  (5 shorter events, 0.0 us)
Async XLA Ops:
  0.0 3.4 %copy-start = (bf16[8,1024,512]{2,1,0:T(8,128)(2,1)S(1)}, bf16[8,1024,512]{2,1,0:T(8,128)(2,1)}, u32[]{:S(2)}) copy-start(bf16[8,1024,512]{2,1,0:T(8,128)(2,1)} %traces.1) | copy-start | bytes 25165828
  3.4 0.8 copy-start.3
  8.7 40.8 %copy-start.6 = (s32[8]{0:T(128)S(1)}, s32[8]{0:T(128)}, u32[]{:S(2)}) copy-start(s32[8]{0:T(128)} %param.10) | copy-start | bytes 100
  8.8 42.3 %copy-start.5 = (f32[2,8]{1,0:T(2,128)S(1)}, f32[2,8]{1,0:T(2,128)}, u32[]{:S(2)}) copy-start(f32[2,8]{1,0:T(2,128)} %param.11) | copy-start | bytes 196
  8.8 42.5 %copy-start.1 = (s32[128,128]{1,0:T(8,128)S(1)}, s32[128,128]{1,0:T(8,128)}, u32[]{:S(2)}) copy-start(s32[128,128]{1,0:T(8,128)} %acquired.3) | copy-start | bytes 196612
  8.8 42.5 %copy-start.4 = (s32[128]{0:T(128)S(1)}, s32[128]{0:T(128)}, u32[]{:S(2)}) copy-start(s32[128]{0:T(128)} %partner.3) | copy-start | bytes 1540
  49.5 4.9 %collective-permute-start = (bf16[128,8,1024]{2,1,0:T(8,128)(2,1)S(1)}, bf16[128,8,1024]{2,1,0:T(8,128)(2,1)}, u32[]{:S(2)}, u32[]{:S(2)}) collective-permute-start(bf16[128,8,1024]{2,1,0:T(8,128)(2,1)S(1)} %all_to_all.10.rows), channel_id=1, source_target_pairs={{0,16},{16,0},{1,17},{17,1},{2,18},{18,2},{3,19},{19,3},{4,20},{20... | collective-permute-start | bytes 6291464 | tf_op jit(solution)/shard_map/ppermute | solution.py:282
  71.8 21.5 %copy-start.2 = (bf16[2,64,512]{2,1,0:T(8,128)(2,1)S(1)}, bf16[2,64,512]{2,1,0:T(8,128)(2,1)}, u32[]{:S(2)}) copy-start(bf16[2,64,512]{2,1,0:T(8,128)(2,1)} %constant.41.clone.tables) | copy-start | bytes 393220

commit v3 on v2

--- a/solution.py
+++ b/solution.py
@@ -17,6 +17,7 @@
 BS = 8
 ITERS = 5
 NB = NS // BS
+NGROUPS = 8
 GROUP = 32
 OWN = GROUP * BS
 ALL_AXES = ("z_hi", "z_lo", "core", "x", "y")
@@ -71,7 +72,7 @@
             pltpu.VMEM((BS, 2 * NF, NS), jnp.float32),
             pltpu.SemaphoreType.DMA((BS + 1,)),
         ],
-        compiler_params=pltpu.CompilerParams(vmem_limit_bytes=24 * 1024 * 1024),
+        compiler_params=pltpu.CompilerParams(vmem_limit_bytes=54 * 1024 * 1024),
         name="transform",
     )(table, traces)
 
@@ -186,8 +187,33 @@
 
 
 def solve_kernel(
-    partner, place, wave, acquired, first, rows, out, mirror, second, factor, left, base, mask
+    partner,
+    place,
+    band_counts,
+    wavelet,
+    acquired,
+    first,
+    rows,
+    out,
+    mirror,
+    second,
+    factor,
+    left,
+    base,
+    mask,
 ):
+    band_end = jnp.int32(0)
+    group = jnp.int32(0)
+    for g in range(NGROUPS):
+        band_end = band_end + band_counts[g]
+        group = group + (band_end <= place[2]).astype(jnp.int32)
+    rescale = 1.0 / math.sqrt(NS)
+    wave_re = wavelet[0, group] * rescale
+    wave_im = wavelet[1, group] * rescale
+    wave = (
+        jnp.where(place[1] == 0, wave_re, -wave_im),
+        jnp.where(place[1] == 0, wave_im, -wave_re),
+    )
     fill(partner, acquired, rows, mirror, mask, second)
 
     def scale(pair, carry):
@@ -249,13 +275,13 @@
         sweep(turn_index % 2, turn_index == ITERS - 1)
 
 
-def solve(partner, place, wave, acquired, first, rows):
+def solve(partner, place, band_counts, wavelet, acquired, first, rows):
     smem = pl.BlockSpec(memory_space=pltpu.SMEM)
     vmem = pl.BlockSpec(memory_space=pltpu.VMEM)
     return pl.pallas_call(
         solve_kernel,
         out_shape=jax.ShapeDtypeStruct((GROUP, 2, BS, NS), jnp.bfloat16),
-        in_specs=[smem, smem, smem, vmem, vmem, vmem],
+        in_specs=[smem, smem, smem, smem, vmem, vmem, vmem],
         out_specs=vmem,
         scratch_shapes=[
             pltpu.VMEM((NB, BS, NS), jnp.bfloat16),
@@ -267,14 +293,14 @@
         ],
         compiler_params=pltpu.CompilerParams(vmem_limit_bytes=32 * 1024 * 1024),
         name="solve",
-    )(partner, place, wave, acquired, first, rows)
+    )(partner, place, band_counts, wavelet, acquired, first, rows)
 
 
 def shards(recorded, acquired, partner, band_counts, wavelet):
     core = lax.axis_index("core")
     z_hi = lax.axis_index("z_hi")
     my_bin = lax.axis_index("z_lo") * 16 + lax.axis_index("x") * 4 + lax.axis_index("y")
-    place = jnp.stack([z_hi * 2, core]).astype(jnp.int32)
+    place = jnp.stack([z_hi * 2, core, my_bin]).astype(jnp.int32)
     forward, inverse = dft_tables()
     ordered = forward.reshape(2, 2, 16, NT).transpose(1, 0, 2, 3).reshape(2 * NF, NT)
     outgoing = transform(jnp.asarray(ordered), recorded)
@@ -282,13 +308,7 @@
     second = lax.ppermute(first, "core", [(0, 1), (1, 0)])
     filled = fill_first(partner, acquired, first)
 
-    band_ends = jnp.cumsum(band_counts)
-    my_group = jnp.sum((band_ends <= my_bin).astype(jnp.int32))
-    chosen = (jnp.arange(8, dtype=jnp.int32) == my_group).astype(jnp.float32)
-    rescale = 1.0 / math.sqrt(NS)
-    wave = jnp.sum(wavelet * chosen[None, :], axis=1) * rescale
-    wave = jnp.where(core == 0, wave, -wave[::-1])
-    estimate = solve(partner, place, wave, acquired, filled, second)
+    estimate = solve(partner, place, band_counts, wavelet, acquired, filled, second)
 
     returned = lax.all_to_all(estimate, BIN_AXES, split_axis=0, concat_axis=0, tiled=True)
     paired = inverse.reshape(2, NF, NT).transpose(1, 0, 2)

time: 98.3 us -> 95.1 us (0.967)
  local copies, waits for them, and re-layouts: 4.35 us -> 0.03 us
  Pallas kernels: 29.4 us -> 31.4 us
  other arithmetic: 1.64 us -> 0.08 us
  waiting for transfers between devices: 0.01 us -> 1.04 us
    unnamed x14 -> x10, local copies, waits for them, and re-layouts: 4.25 us -> 0.03 us
    pallas_call x1, Pallas kernels: 4.51 us -> 6.48 us  [transform(): pl.pallas_call(transform_kernel, out_shape=jax.ShapeDtypeStruct((NB, BS,...]
    ppermute x1, waiting for transfers between devices: 0.01 us -> 1.04 us  [shards(): second = lax.ppermute(first, 'core', [(0, 1), (1, 0)])]
  transfers between devices with their start and end apart: 1 -> 1, of which waited for: 0 -> 1; matrix products, arithmetic and copies ran while one was open for 2% -> 0% of each run, Pallas kernels for 3% -> 3%
where the time goes in v3:
time: 95.1 us; the launch traced here: 94.8 us
  blocking collectives  62 us (65%)
  Pallas kernels  31.4 us (33%)
  waiting for transfers between devices  1.04 us (1%)
    all_to_all x1, blocking collectives, shards(): lax.all_to_all(outgoing, ALL_AXES, split_axis=0, concat_axis=0, tiled=True)  41 us
    all_to_all x1, blocking collectives, shards(): lax.all_to_all(estimate, BIN_AXES, split_axis=0, concat_axis=0, tiled=True)  21.1 us
    pallas_call x1, Pallas kernels, solve(): pl.pallas_call(solve_kernel, out_shape=jax.ShapeDtypeStruct((GROUP, 2, BS...  17.3 us
    pallas_call x1, Pallas kernels, transform(): pl.pallas_call(transform_kernel, out_shape=jax.ShapeDtypeStruct((NB, BS,...  6.48 us
    pallas_call x1, Pallas kernels, restore(): pl.pallas_call(restore_kernel, out_shape=jax.ShapeDtypeStruct((BS, NS, NT...  4.43 us
    pallas_call x1, Pallas kernels, fill_first(): pl.pallas_call(fill_first_kernel, out_shape=jax.ShapeDtypeStruct((NS, NS)...  3.15 us
  transfers between devices with their start and end apart: 1, of which 1 were waited for; matrix products, arithmetic and copies ran while one was open for 0% of the time, Pallas kernels for 3%

profile of v3, /device:TPU:0, one launch (start us, length us, event | category | flops | bytes accessed | tf_op | source)
XLA Modules:
  0.0 94.8 jit_solution(12462522162526987961)
XLA Ops:
  0.0 6.5 %transform.1 = bf16[128,8,1024]{2,1,0:T(8,128)(2,1)} custom-call(bf16[64,512]{1,0:T(8,128)(2,1)} %constant.31.clone.table_from, bf16[8,1024,512]{2,1,0:T(8,128)(2,1)} %traces.1), custom_call_target="tpu_custom_call" | custom-call | tf_op jit(solution)/shard_map/transform/pallas_call | solution.py:64
  6.5 0.0 copy-start
  6.5 0.0 copy-start.2
  6.5 41.0 %all_to_all.10.rows = bf16[128,8,1024]{2,1,0:T(8,128)(2,1)S(1)} all-to-all(bf16[128,8,1024]{2,1,0:T(8,128)(2,1)} %transform.1), channel_id=1, replica_groups=mesh['z_hi'=2,'z_lo'=2,'core'=2,'x'=4,'y'=4] {'z_hi','z_lo','core','x','y'}, dimensions={0} | all-to-all | bytes 4194304 | tf_op jit(solution)/shard_map/all_to_all | solution.py:307
  47.5 0.0 collective-permute-start
  47.5 0.1 pad_add_fusion.place
  47.6 0.0 copy-done
  47.6 0.0 copy-done.2
  47.6 0.0 copy-start.3
  47.6 0.0 copy-start.4
  47.6 3.1 %fill_first.1.first = bf16[1024,1024]{1,0:T(8,128)(2,1)S(1)} custom-call(s32[128]{0:T(128)S(1)} %copy-done.2, s32[128,128]{1,0:T(8,128)S(1)} %copy-done, bf16[128,8,1024]{2,1,0:T(8,128)(2,1)S(1)} %all_to_all.10.rows), custom_call_target="tpu_custom_call" | custom-call | tf_op jit(solution)/shard_map/fill_first/pallas_call | solution.py:175
  50.7 1.0 %collective-permute-done.rows = bf16[128,8,1024]{2,1,0:T(8,128)(2,1)} collective-permute-done((bf16[128,8,1024]{2,1,0:T(8,128)(2,1)S(1)}, bf16[128,8,1024]{2,1,0:T(8,128)(2,1)}, u32[]{:S(2)}, u32[]{:S(2)}) %collective-permute-start) | collective-permute-done | bytes 2097184 | tf_op jit(solution)/shard_map/ppermute | solution.py:308
  51.8 0.0 copy-done.3
  51.8 0.0 copy-done.4
  51.8 17.3 %solve.1 = bf16[32,2,8,1024]{3,2,1,0:T(8,128)(2,1)S(1)} custom-call(s32[128]{0:T(128)S(1)} %copy-done.2, s32[3]{0:T(128)S(1)} %pad_add_fusion.place, s32[8]{0:T(128)S(1)} %copy-done.4, f32[2,8]{1,0:T(2,128)S(1)} %copy-done.3, s32[128,128]{1,0:T(8,128)S(1)} %copy-done, bf16[1024,1024]{1,0:T(8,128)(2,1)S(1)} %fill_first.1.first, ...), custom_call_target="tpu_custom_call" | custom-call | tf_op jit(solution)/shard_map/solve/pallas_call | solution.py:281
  69.1 0.0 copy-start.1
  69.1 21.1 %all_to_all.11.spectra = bf16[32,2,8,1024]{3,2,1,0:T(8,128)(2,1)S(1)} all-to-all(bf16[32,2,8,1024]{3,2,1,0:T(8,128)(2,1)S(1)} %solve.1), channel_id=1, replica_groups=mesh['z_hi'=2,'z_lo'=2,'core'=2,'x'=4,'y'=4] {'z_lo','x','y'}, dimensions={0} | all-to-all | bytes 2097152 | tf_op jit(solution)/shard_map/all_to_all | solution.py:313
  90.2 0.0 copy-done.1
  90.2 4.4 %restore.1 = bf16[8,1024,512]{2,1,0:T(8,128)(2,1)} custom-call(s32[3]{0:T(128)S(1)} %pad_add_fusion.place, bf16[32,2,8,1024]{3,2,1,0:T(8,128)(2,1)S(1)} %all_to_all.11.spectra, bf16[2,64,512]{2,1,0:T(8,128)(2,1)S(1)} %copy-done.1), custom_call_target="tpu_custom_call" | custom-call | tf_op jit(solution)/shard_map/restore/pallas_call | solution.py:101
Async XLA Ops:
  6.5 41.1 %copy-start = (s32[128,128]{1,0:T(8,128)S(1)}, s32[128,128]{1,0:T(8,128)}, u32[]{:S(2)}) copy-start(s32[128,128]{1,0:T(8,128)} %acquired.3) | copy-start | bytes 196612
  6.5 41.1 %copy-start.2 = (s32[128]{0:T(128)S(1)}, s32[128]{0:T(128)}, u32[]{:S(2)}) copy-start(s32[128]{0:T(128)} %partner.3) | copy-start | bytes 1540
  47.5 4.3 %collective-permute-start = (bf16[128,8,1024]{2,1,0:T(8,128)(2,1)S(1)}, bf16[128,8,1024]{2,1,0:T(8,128)(2,1)}, u32[]{:S(2)}, u32[]{:S(2)}) collective-permute-start(bf16[128,8,1024]{2,1,0:T(8,128)(2,1)S(1)} %all_to_all.10.rows), channel_id=1, source_target_pairs={{0,16},{16,0},{1,17},{17,1},{2,18},{18,2},{3,19},{19,3},{4,20},{20... | collective-permute-start | bytes 6291464 | tf_op jit(solution)/shard_map/ppermute | solution.py:308
  47.6 4.2 %copy-start.3 = (f32[2,8]{1,0:T(2,128)S(1)}, f32[2,8]{1,0:T(2,128)}, u32[]{:S(2)}) copy-start(f32[2,8]{1,0:T(2,128)} %wavelet.1) | copy-start | bytes 196
  47.6 4.2 %copy-start.4 = (s32[8]{0:T(128)S(1)}, s32[8]{0:T(128)}, u32[]{:S(2)}) copy-start(s32[8]{0:T(128)} %band_counts.1) | copy-start | bytes 100
  69.1 21.1 %copy-start.1 = (bf16[2,64,512]{2,1,0:T(8,128)(2,1)S(1)}, bf16[2,64,512]{2,1,0:T(8,128)(2,1)}, u32[]{:S(2)}) copy-start(bf16[2,64,512]{2,1,0:T(8,128)(2,1)} %constant.32.clone.tables) | copy-start | bytes 393220

commit v4 on v3

--- a/solution.py
+++ b/solution.py
@@ -113,7 +113,7 @@
     )(place, spectra, tables)
 
 
-def fill(partner, acquired, rows, mirror, mask, filled):
+def spread(acquired, mask):
     column_block = lax.broadcasted_iota(jnp.int32, (NB, NS), 1) // BS
     expand = (column_block == lax.broadcasted_iota(jnp.int32, (NB, NS), 0)).astype(jnp.bfloat16)
     mask[...] = jnp.dot(
@@ -121,6 +121,9 @@
         expand,
         preferred_element_type=jnp.float32,
     )
+
+
+def turn(partner, rows, mirror):
     size = 256
     identity = (
         lax.broadcasted_iota(jnp.int32, (size, size), 0)
@@ -147,27 +150,29 @@
                 group * size : (group + 1) * size,
             ] = turned.reshape(size // BS, BS, size).astype(jnp.bfloat16)
 
-    def choose(pair, carry):
-        blocks = []
-        for i in range(2):
-            block = pair * 2 + i
-            keep = mask[pl.ds(block, 1), :] > 0.5
-            blocks.append(
-                jnp.where(
-                    keep,
-                    rows[source_of(block)].astype(jnp.float32),
-                    mirror[partner[block]].astype(jnp.float32),
-                )
-            )
+
+def choose(partner, rows, mirror, mask, block, columns):
+    keep = mask[pl.ds(block, 1), columns] > 0.5
+    return jnp.where(
+        keep,
+        rows[source_of(block), :, columns].astype(jnp.float32),
+        mirror[partner[block], :, columns].astype(jnp.float32),
+    )
+
+
+def fill_first_kernel(partner, acquired, rows, filled, mirror, mask):
+    spread(acquired, mask)
+    turn(partner, rows, mirror)
+
+    def pick(pair, carry):
+        blocks = [
+            choose(partner, rows, mirror, mask, pair * 2 + i, slice(None)) for i in range(2)
+        ]
         row = pl.multiple_of(pair * 16, 16)
         filled[pl.ds(row, 16), :] = jnp.concatenate(blocks, axis=0).astype(jnp.bfloat16)
         return carry
 
-    lax.fori_loop(0, NB // 2, choose, 0, unroll=8)
-
-
-def fill_first_kernel(partner, acquired, rows, filled, mirror, mask):
-    fill(partner, acquired, rows, mirror, mask, filled)
+    lax.fori_loop(0, NB // 2, pick, 0, unroll=8)
 
 
 def fill_first(partner, acquired, rows):
@@ -196,7 +201,6 @@
     rows,
     out,
     mirror,
-    second,
     factor,
     left,
     base,
@@ -214,17 +218,23 @@
         jnp.where(place[1] == 0, wave_re, -wave_im),
         jnp.where(place[1] == 0, wave_im, -wave_re),
     )
-    fill(partner, acquired, rows, mirror, mask, second)
-
-    def scale(pair, carry):
-        row = pl.multiple_of(pair * 16, 16)
-        real = first[pl.ds(row, 16), :].astype(jnp.float32)
-        imag = second[pl.ds(row, 16), :].astype(jnp.float32)
-        factor[pl.ds(row, 16), :] = (wave[0] * real - wave[1] * imag).astype(jnp.bfloat16)
-        factor[pl.ds(NS + row, 16), :] = (wave[0] * imag + wave[1] * real).astype(jnp.bfloat16)
-        return carry
-
-    lax.fori_loop(0, NB // 2, scale, 0, unroll=8)
+    spread(acquired, mask)
+    turn(partner, rows, mirror)
+
+    def scale(columns):
+        for pair in range(NB // 2):
+            row = pair * 16
+            real = first[row : row + 16, columns].astype(jnp.float32)
+            imag = jnp.concatenate(
+                [choose(partner, rows, mirror, mask, pair * 2 + i, columns) for i in range(2)],
+                axis=0,
+            )
+            factor[row : row + 16, columns] = (wave[0] * real - wave[1] * imag).astype(
+                jnp.bfloat16
+            )
+            factor[NS + row : NS + row + 16, columns] = (
+                wave[0] * imag + wave[1] * real
+            ).astype(jnp.bfloat16)
 
     def put(slot, row, rows, real, imag, column, columns):
         real_low = real.astype(jnp.bfloat16)
@@ -235,28 +245,32 @@
         left[slot, pl.ds(OWN + row, rows), pl.ds(NS + column, columns)] = real_low
 
     def own(pair, carry):
-        values = []
-        for part in (first, second):
-            blocks = []
-            for i in range(2):
-                member = pair * 2 + i
-                chip = (member % 16) * 4 + member // 16 + place[0]
-                both = part[pl.ds(pl.multiple_of(chip * 16, 16), 16), :].astype(jnp.float32)
-                blocks.append(jnp.where(place[1] == 0, both[:BS], both[BS:]))
-            values.append(jnp.concatenate(blocks, axis=0))
+        reals, imags = [], []
+        for i in range(2):
+            member = pair * 2 + i
+            chip = (member % 16) * 4 + member // 16 + place[0]
+            both = first[pl.ds(pl.multiple_of(chip * 16, 16), 16), :].astype(jnp.float32)
+            reals.append(jnp.where(place[1] == 0, both[:BS], both[BS:]))
+            imags.append(
+                choose(partner, rows, mirror, mask, chip * 2 + place[1], slice(None))
+            )
+        real = jnp.concatenate(reals, axis=0)
+        imag = jnp.concatenate(imags, axis=0)
         row = pl.multiple_of(pair * 16, 16)
-        base[pl.ds(row, 16), :] = values[0]
-        base[pl.ds(OWN + row, 16), :] = values[1]
-        put(0, row, 16, values[0], values[1], 0, NS)
+        base[pl.ds(row, 16), :] = real
+        base[pl.ds(OWN + row, 16), :] = imag
+        put(0, row, 16, real, imag, 0, NS)
         return carry
 
     lax.fori_loop(0, GROUP // 2, own, 0, unroll=4)
 
     width = 256
 
-    def sweep(slot, last):
+    def sweep(slot, first_turn, last):
         for tile in range(NS // width):
-            columns = pl.ds(tile * width, width)
+            columns = slice(tile * width, (tile + 1) * width)
+            if first_turn:
+                scale(columns)
             product = jnp.dot(
                 left[slot], factor[:, columns], preferred_element_type=jnp.float32
             )
@@ -272,7 +286,7 @@
                 put(1 - slot, 0, OWN, value[:OWN], value[OWN:], tile * width, width)
 
     for turn_index in range(ITERS):
-        sweep(turn_index % 2, turn_index == ITERS - 1)
+        sweep(turn_index % 2, turn_index == 0, turn_index == ITERS - 1)
 
 
 def solve(partner, place, band_counts, wavelet, acquired, first, rows):
@@ -285,7 +299,6 @@
         out_specs=vmem,
         scratch_shapes=[
             pltpu.VMEM((NB, BS, NS), jnp.bfloat16),
-            pltpu.VMEM((NS, NS), jnp.bfloat16),
             pltpu.VMEM((2 * NS, NS), jnp.bfloat16),
             pltpu.VMEM((2, 2 * OWN, 2 * NS), jnp.bfloat16),
             pltpu.VMEM((2 * OWN, NS), jnp.float32),

time: 95.1 us -> 93.1 us (0.979)
  Pallas kernels: 31.4 us -> 29.4 us
    pallas_call x1, Pallas kernels: 17.3 us -> 15.3 us  [solve(): pl.pallas_call(solve_kernel, out_shape=jax.ShapeDtypeStruct((GROUP, 2, BS...]
where the time goes in v4:
time: 93.1 us; the launch traced here: 92.8 us
  blocking collectives  62 us (67%)
  Pallas kernels  29.4 us (32%)
  waiting for transfers between devices  1.03 us (1%)
    all_to_all x1, blocking collectives, shards(): lax.all_to_all(outgoing, ALL_AXES, split_axis=0, concat_axis=0, tiled=True)  41 us
    all_to_all x1, blocking collectives, shards(): lax.all_to_all(estimate, BIN_AXES, split_axis=0, concat_axis=0, tiled=True)  21.1 us
    pallas_call x1, Pallas kernels, solve(): pl.pallas_call(solve_kernel, out_shape=jax.ShapeDtypeStruct((GROUP, 2, BS...  15.3 us
    pallas_call x1, Pallas kernels, transform(): pl.pallas_call(transform_kernel, out_shape=jax.ShapeDtypeStruct((NB, BS,...  6.48 us
    pallas_call x1, Pallas kernels, restore(): pl.pallas_call(restore_kernel, out_shape=jax.ShapeDtypeStruct((BS, NS, NT...  4.42 us
    pallas_call x1, Pallas kernels, fill_first(): pl.pallas_call(fill_first_kernel, out_shape=jax.ShapeDtypeStruct((NS, NS)...  3.15 us
  transfers between devices with their start and end apart: 1, of which 1 were waited for; matrix products, arithmetic and copies ran while one was open for 0% of the time, Pallas kernels for 3%

profile of v4, /device:TPU:0, one launch (start us, length us, event | category | flops | bytes accessed | tf_op | source)
XLA Modules:
  0.0 92.8 jit_solution(16721379889666543734)
XLA Ops:
  0.0 6.5 %transform.1 = bf16[128,8,1024]{2,1,0:T(8,128)(2,1)} custom-call(bf16[64,512]{1,0:T(8,128)(2,1)} %constant.31.clone.table_from, bf16[8,1024,512]{2,1,0:T(8,128)(2,1)} %traces.1), custom_call_target="tpu_custom_call" | custom-call | tf_op jit(solution)/shard_map/transform/pallas_call | solution.py:64
  6.5 0.0 copy-start
  6.5 0.0 copy-start.2
  6.5 41.0 %all_to_all.10.rows = bf16[128,8,1024]{2,1,0:T(8,128)(2,1)S(1)} all-to-all(bf16[128,8,1024]{2,1,0:T(8,128)(2,1)} %transform.1), channel_id=1, replica_groups=mesh['z_hi'=2,'z_lo'=2,'core'=2,'x'=4,'y'=4] {'z_hi','z_lo','core','x','y'}, dimensions={0} | all-to-all | bytes 4194304 | tf_op jit(solution)/shard_map/all_to_all | solution.py:320
  47.5 0.0 collective-permute-start
  47.5 0.1 pad_add_fusion.place
  47.6 0.0 copy-done
  47.6 0.0 copy-done.2
  47.6 0.0 copy-start.3
  47.6 0.0 copy-start.4
  47.6 3.1 %fill_first.1.first = bf16[1024,1024]{1,0:T(8,128)(2,1)S(1)} custom-call(s32[128]{0:T(128)S(1)} %copy-done.2, s32[128,128]{1,0:T(8,128)S(1)} %copy-done, bf16[128,8,1024]{2,1,0:T(8,128)(2,1)S(1)} %all_to_all.10.rows), custom_call_target="tpu_custom_call" | custom-call | tf_op jit(solution)/shard_map/fill_first/pallas_call | solution.py:180
  50.7 1.0 %collective-permute-done.rows = bf16[128,8,1024]{2,1,0:T(8,128)(2,1)} collective-permute-done((bf16[128,8,1024]{2,1,0:T(8,128)(2,1)S(1)}, bf16[128,8,1024]{2,1,0:T(8,128)(2,1)}, u32[]{:S(2)}, u32[]{:S(2)}) %collective-permute-start) | collective-permute-done | bytes 2097184 | tf_op jit(solution)/shard_map/ppermute | solution.py:321
  51.8 0.0 copy-done.3
  51.8 0.0 copy-done.4
  51.8 15.3 %solve.1 = bf16[32,2,8,1024]{3,2,1,0:T(8,128)(2,1)S(1)} custom-call(s32[128]{0:T(128)S(1)} %copy-done.2, s32[3]{0:T(128)S(1)} %pad_add_fusion.place, s32[8]{0:T(128)S(1)} %copy-done.4, f32[2,8]{1,0:T(2,128)S(1)} %copy-done.3, s32[128,128]{1,0:T(8,128)S(1)} %copy-done, bf16[1024,1024]{1,0:T(8,128)(2,1)S(1)} %fill_first.1.first, ...), custom_call_target="tpu_custom_call" | custom-call | tf_op jit(solution)/shard_map/solve/pallas_call | solution.py:295
  67.1 0.0 copy-start.1
  67.1 21.1 %all_to_all.11.spectra = bf16[32,2,8,1024]{3,2,1,0:T(8,128)(2,1)S(1)} all-to-all(bf16[32,2,8,1024]{3,2,1,0:T(8,128)(2,1)S(1)} %solve.1), channel_id=1, replica_groups=mesh['z_hi'=2,'z_lo'=2,'core'=2,'x'=4,'y'=4] {'z_lo','x','y'}, dimensions={0} | all-to-all | bytes 2097152 | tf_op jit(solution)/shard_map/all_to_all | solution.py:326
  88.2 0.0 copy-done.1
  88.2 4.4 %restore.1 = bf16[8,1024,512]{2,1,0:T(8,128)(2,1)} custom-call(s32[3]{0:T(128)S(1)} %pad_add_fusion.place, bf16[32,2,8,1024]{3,2,1,0:T(8,128)(2,1)S(1)} %all_to_all.11.spectra, bf16[2,64,512]{2,1,0:T(8,128)(2,1)S(1)} %copy-done.1), custom_call_target="tpu_custom_call" | custom-call | tf_op jit(solution)/shard_map/restore/pallas_call | solution.py:101
Async XLA Ops:
  6.5 41.1 %copy-start = (s32[128,128]{1,0:T(8,128)S(1)}, s32[128,128]{1,0:T(8,128)}, u32[]{:S(2)}) copy-start(s32[128,128]{1,0:T(8,128)} %acquired.3) | copy-start | bytes 196612
  6.5 41.1 %copy-start.2 = (s32[128]{0:T(128)S(1)}, s32[128]{0:T(128)}, u32[]{:S(2)}) copy-start(s32[128]{0:T(128)} %partner.3) | copy-start | bytes 1540
  47.5 4.3 %collective-permute-start = (bf16[128,8,1024]{2,1,0:T(8,128)(2,1)S(1)}, bf16[128,8,1024]{2,1,0:T(8,128)(2,1)}, u32[]{:S(2)}, u32[]{:S(2)}) collective-permute-start(bf16[128,8,1024]{2,1,0:T(8,128)(2,1)S(1)} %all_to_all.10.rows), channel_id=1, source_target_pairs={{0,16},{16,0},{1,17},{17,1},{2,18},{18,2},{3,19},{19,3},{4,20},{20... | collective-permute-start | bytes 6291464 | tf_op jit(solution)/shard_map/ppermute | solution.py:321
  47.6 4.2 %copy-start.3 = (f32[2,8]{1,0:T(2,128)S(1)}, f32[2,8]{1,0:T(2,128)}, u32[]{:S(2)}) copy-start(f32[2,8]{1,0:T(2,128)} %wavelet.1) | copy-start | bytes 196
  47.6 4.2 %copy-start.4 = (s32[8]{0:T(128)S(1)}, s32[8]{0:T(128)}, u32[]{:S(2)}) copy-start(s32[8]{0:T(128)} %band_counts.1) | copy-start | bytes 100
  67.1 21.1 %copy-start.1 = (bf16[2,64,512]{2,1,0:T(8,128)(2,1)S(1)}, bf16[2,64,512]{2,1,0:T(8,128)(2,1)}, u32[]{:S(2)}) copy-start(bf16[2,64,512]{2,1,0:T(8,128)(2,1)} %constant.32.clone.tables) | copy-start | bytes 393220

commit v5 on v4

--- a/solution.py
+++ b/solution.py
@@ -72,7 +72,7 @@
             pltpu.VMEM((BS, 2 * NF, NS), jnp.float32),
             pltpu.SemaphoreType.DMA((BS + 1,)),
         ],
-        compiler_params=pltpu.CompilerParams(vmem_limit_bytes=54 * 1024 * 1024),
+        compiler_params=pltpu.CompilerParams(vmem_limit_bytes=24 * 1024 * 1024),
         name="transform",
     )(table, traces)
 
@@ -160,7 +160,7 @@
     )
 
 
-def fill_first_kernel(partner, acquired, rows, filled, mirror, mask):
+def fill_first_kernel(partner, acquired, rows, filled, mask, mirror):
     spread(acquired, mask)
     turn(partner, rows, mirror)
 
@@ -179,13 +179,13 @@
     vmem = pl.BlockSpec(memory_space=pltpu.VMEM)
     return pl.pallas_call(
         fill_first_kernel,
-        out_shape=jax.ShapeDtypeStruct((NS, NS), jnp.bfloat16),
+        out_shape=(
+            jax.ShapeDtypeStruct((NS, NS), jnp.bfloat16),
+            jax.ShapeDtypeStruct((NB, NS), jnp.float32),
+        ),
         in_specs=[pl.BlockSpec(memory_space=pltpu.SMEM), vmem, vmem],
-        out_specs=vmem,
-        scratch_shapes=[
-            pltpu.VMEM((NB, BS, NS), jnp.bfloat16),
-            pltpu.VMEM((NB, NS), jnp.float32),
-        ],
+        out_specs=(vmem, vmem),
+        scratch_shapes=[pltpu.VMEM((NB, BS, NS), jnp.bfloat16)],
         compiler_params=pltpu.CompilerParams(vmem_limit_bytes=16 * 1024 * 1024),
         name="fill_first",
     )(partner, acquired, rows)
@@ -196,7 +196,7 @@
     place,
     band_counts,
     wavelet,
-    acquired,
+    mask,
     first,
     rows,
     out,
@@ -204,7 +204,6 @@
     factor,
     left,
     base,
-    mask,
 ):
     band_end = jnp.int32(0)
     group = jnp.int32(0)
@@ -218,7 +217,6 @@
         jnp.where(place[1] == 0, wave_re, -wave_im),
         jnp.where(place[1] == 0, wave_im, -wave_re),
     )
-    spread(acquired, mask)
     turn(partner, rows, mirror)
 
     def scale(columns):
@@ -289,7 +287,7 @@
         sweep(turn_index % 2, turn_index == 0, turn_index == ITERS - 1)
 
 
-def solve(partner, place, band_counts, wavelet, acquired, first, rows):
+def solve(partner, place, band_counts, wavelet, mask, first, rows):
     smem = pl.BlockSpec(memory_space=pltpu.SMEM)
     vmem = pl.BlockSpec(memory_space=pltpu.VMEM)
     return pl.pallas_call(
@@ -302,11 +300,10 @@
             pltpu.VMEM((2 * NS, NS), jnp.bfloat16),
             pltpu.VMEM((2, 2 * OWN, 2 * NS), jnp.bfloat16),
             pltpu.VMEM((2 * OWN, NS), jnp.float32),
-            pltpu.VMEM((NB, NS), jnp.float32),
         ],
         compiler_params=pltpu.CompilerParams(vmem_limit_bytes=32 * 1024 * 1024),
         name="solve",
-    )(partner, place, band_counts, wavelet, acquired, first, rows)
+    )(partner, place, band_counts, wavelet, mask, first, rows)
 
 
 def shards(recorded, acquired, partner, band_counts, wavelet):
@@ -316,12 +313,15 @@
     place = jnp.stack([z_hi * 2, core, my_bin]).astype(jnp.int32)
     forward, inverse = dft_tables()
     ordered = forward.reshape(2, 2, 16, NT).transpose(1, 0, 2, 3).reshape(2 * NF, NT)
-    outgoing = transform(jnp.asarray(ordered), recorded)
+    outgoing = transform(
+        pltpu.with_memory_space_constraint(jnp.asarray(ordered), pltpu.HBM),
+        pltpu.with_memory_space_constraint(recorded, pltpu.HBM),
+    )
     first = lax.all_to_all(outgoing, ALL_AXES, split_axis=0, concat_axis=0, tiled=True)
     second = lax.ppermute(first, "core", [(0, 1), (1, 0)])
-    filled = fill_first(partner, acquired, first)
-
-    estimate = solve(partner, place, band_counts, wavelet, acquired, filled, second)
+    filled, mask = fill_first(partner, acquired, first)
+
+    estimate = solve(partner, place, band_counts, wavelet, mask, filled, second)
 
     returned = lax.all_to_all(estimate, BIN_AXES, split_axis=0, concat_axis=0, tiled=True)
     paired = inverse.reshape(2, NF, NT).transpose(1, 0, 2)

time: 93.1 us -> 91.4 us (0.982)
  Pallas kernels: 29.4 us -> 28 us
    pallas_call x1, Pallas kernels: 6.48 us -> 5.15 us  [transform(): pl.pallas_call(transform_kernel, out_shape=jax.ShapeDtypeStruct((NB, BS,...]
where the time goes in v5:
time: 91.4 us; the launch traced here: 91.2 us
  blocking collectives  61.8 us (68%)
  Pallas kernels  28 us (31%)
  waiting for transfers between devices  1.07 us (1%)
    all_to_all x1, blocking collectives, shards(): lax.all_to_all(outgoing, ALL_AXES, split_axis=0, concat_axis=0, tiled=True)  40.8 us
    all_to_all x1, blocking collectives, shards(): lax.all_to_all(estimate, BIN_AXES, split_axis=0, concat_axis=0, tiled=True)  21.1 us
    pallas_call x1, Pallas kernels, solve(): pl.pallas_call(solve_kernel, out_shape=jax.ShapeDtypeStruct((GROUP, 2, BS...  15.3 us
    pallas_call x1, Pallas kernels, transform(): pl.pallas_call(transform_kernel, out_shape=jax.ShapeDtypeStruct((NB, BS,...  5.15 us
    pallas_call x1, Pallas kernels, restore(): pl.pallas_call(restore_kernel, out_shape=jax.ShapeDtypeStruct((BS, NS, NT...  4.42 us
    pallas_call x1, Pallas kernels, fill_first(): pl.pallas_call(fill_first_kernel, out_shape=(jax.ShapeDtypeStruct((NS, NS...  3.11 us
  transfers between devices with their start and end apart: 1, of which 1 were waited for; matrix products, arithmetic and copies ran while one was open for 0% of the time, Pallas kernels for 3%

profile of v5, /device:TPU:0, one launch (start us, length us, event | category | flops | bytes accessed | tf_op | source)
XLA Modules:
  0.0 91.2 jit_solution(16327055417721577941)
XLA Ops:
  0.0 5.2 %transform.1 = bf16[128,8,1024]{2,1,0:T(8,128)(2,1)S(1)} custom-call(bf16[64,512]{1,0:T(8,128)(2,1)} %constant.31.clone.table_from, bf16[8,1024,512]{2,1,0:T(8,128)(2,1)} %traces.1), custom_call_target="tpu_custom_call" | custom-call | tf_op jit(solution)/shard_map/transform/pallas_call | solution.py:64
  5.2 0.0 copy-start.1
  5.2 0.0 copy-start.2
  5.2 40.8 %all_to_all.10.rows = bf16[128,8,1024]{2,1,0:T(8,128)(2,1)S(1)} all-to-all(bf16[128,8,1024]{2,1,0:T(8,128)(2,1)S(1)} %transform.1), channel_id=1, replica_groups=mesh['z_hi'=2,'z_lo'=2,'core'=2,'x'=4,'y'=4] {'z_hi','z_lo','core','x','y'}, dimensions={0} | all-to-all | bytes 4194304 | tf_op jit(solution)/shard_map/all_to_all | solution.py:320
  45.9 0.0 copy-start.3
  45.9 0.0 copy-start.4
  45.9 0.0 collective-permute-start
  46.0 0.1 pad_add_fusion.place
  46.0 0.0 copy-done.1
  46.0 0.0 copy-done.2
  46.0 3.1 %fill_first.1 = (bf16[1024,1024]{1,0:T(8,128)(2,1)S(1)}, f32[128,1024]{1,0:T(8,128)S(1)}) custom-call(s32[128]{0:T(128)S(1)} %copy-done.2, s32[128,128]{1,0:T(8,128)S(1)} %copy-done.1, bf16[128,8,1024]{2,1,0:T(8,128)(2,1)S(1)} %all_to_all.10.rows), custom_call_target="tpu_custom_call" | custom-call | tf_op jit(solution)/shard_map/fill_first/pallas_call | solution.py:180
  49.2 1.1 %collective-permute-done.rows = bf16[128,8,1024]{2,1,0:T(8,128)(2,1)} collective-permute-done((bf16[128,8,1024]{2,1,0:T(8,128)(2,1)S(1)}, bf16[128,8,1024]{2,1,0:T(8,128)(2,1)}, u32[]{:S(2)}, u32[]{:S(2)}) %collective-permute-start) | collective-permute-done | bytes 2097184 | tf_op jit(solution)/shard_map/ppermute | solution.py:321
  50.2 0.0 copy-done.3
  50.2 0.0 copy-done.4
  50.2 15.3 %solve.1 = bf16[32,2,8,1024]{3,2,1,0:T(8,128)(2,1)S(1)} custom-call(s32[128]{0:T(128)S(1)} %copy-done.2, s32[3]{0:T(128)S(1)} %pad_add_fusion.place, s32[8]{0:T(128)S(1)} %copy-done.4, f32[2,8]{1,0:T(2,128)S(1)} %copy-done.3, f32[128,1024]{1,0:T(8,128)S(1)} %get-tuple-element.7.mask, bf16[1024,1024]{1,0:T(8,128)(2,1)S(1)} %get-tuple-element.8.first, ...), custom_call_target="tpu_custom_call" | custom-call | tf_op jit(solution)/shard_map/solve/pallas_call | solution.py:293
  65.5 0.0 copy-start
  65.5 21.1 %all_to_all.11.spectra = bf16[32,2,8,1024]{3,2,1,0:T(8,128)(2,1)S(1)} all-to-all(bf16[32,2,8,1024]{3,2,1,0:T(8,128)(2,1)S(1)} %solve.1), channel_id=1, replica_groups=mesh['z_hi'=2,'z_lo'=2,'core'=2,'x'=4,'y'=4] {'z_lo','x','y'}, dimensions={0} | all-to-all | bytes 2097152 | tf_op jit(solution)/shard_map/all_to_all | solution.py:326
  86.6 0.0 copy-done
  86.6 4.4 %restore.1 = bf16[8,1024,512]{2,1,0:T(8,128)(2,1)} custom-call(s32[3]{0:T(128)S(1)} %pad_add_fusion.place, bf16[32,2,8,1024]{3,2,1,0:T(8,128)(2,1)S(1)} %all_to_all.11.spectra, bf16[2,64,512]{2,1,0:T(8,128)(2,1)S(1)} %copy-done), custom_call_target="tpu_custom_call" | custom-call | tf_op jit(solution)/shard_map/restore/pallas_call | solution.py:101
Async XLA Ops:
  5.2 40.9 %copy-start.1 = (s32[128,128]{1,0:T(8,128)S(1)}, s32[128,128]{1,0:T(8,128)}, u32[]{:S(2)}) copy-start(s32[128,128]{1,0:T(8,128)} %acquired.1) | copy-start | bytes 196612
  5.2 40.9 %copy-start.2 = (s32[128]{0:T(128)S(1)}, s32[128]{0:T(128)}, u32[]{:S(2)}) copy-start(s32[128]{0:T(128)} %partner.3) | copy-start | bytes 1540
  45.9 4.3 %copy-start.3 = (f32[2,8]{1,0:T(2,128)S(1)}, f32[2,8]{1,0:T(2,128)}, u32[]{:S(2)}) copy-start(f32[2,8]{1,0:T(2,128)} %wavelet.1) | copy-start | bytes 196
  45.9 4.3 %copy-start.4 = (s32[8]{0:T(128)S(1)}, s32[8]{0:T(128)}, u32[]{:S(2)}) copy-start(s32[8]{0:T(128)} %band_counts.1) | copy-start | bytes 100
  45.9 4.3 %collective-permute-start = (bf16[128,8,1024]{2,1,0:T(8,128)(2,1)S(1)}, bf16[128,8,1024]{2,1,0:T(8,128)(2,1)}, u32[]{:S(2)}, u32[]{:S(2)}) collective-permute-start(bf16[128,8,1024]{2,1,0:T(8,128)(2,1)S(1)} %all_to_all.10.rows), channel_id=1, source_target_pairs={{0,16},{16,0},{1,17},{17,1},{2,18},{18,2},{3,19},{19,3},{4,20},{20... | collective-permute-start | bytes 6291464 | tf_op jit(solution)/shard_map/ppermute | solution.py:321
  65.5 21.1 %copy-start = (bf16[2,64,512]{2,1,0:T(8,128)(2,1)S(1)}, bf16[2,64,512]{2,1,0:T(8,128)(2,1)}, u32[]{:S(2)}) copy-start(bf16[2,64,512]{2,1,0:T(8,128)(2,1)} %constant.32.clone.tables) | copy-start | bytes 393220

commit v6 on v5

--- a/solution.py
+++ b/solution.py
@@ -148,7 +148,7 @@
                 tile * (size // BS) : (tile + 1) * (size // BS),
                 :,
                 group * size : (group + 1) * size,
-            ] = turned.reshape(size // BS, BS, size).astype(jnp.bfloat16)
+            ] = turned.reshape(size // BS, BS, size)
 
 
 def choose(partner, rows, mirror, mask, block, columns):
@@ -156,7 +156,7 @@
     return jnp.where(
         keep,
         rows[source_of(block), :, columns].astype(jnp.float32),
-        mirror[partner[block], :, columns].astype(jnp.float32),
+        mirror[partner[block], :, columns],
     )
 
 
@@ -185,7 +185,7 @@
         ),
         in_specs=[pl.BlockSpec(memory_space=pltpu.SMEM), vmem, vmem],
         out_specs=(vmem, vmem),
-        scratch_shapes=[pltpu.VMEM((NB, BS, NS), jnp.bfloat16)],
+        scratch_shapes=[pltpu.VMEM((NB, BS, NS), jnp.float32)],
         compiler_params=pltpu.CompilerParams(vmem_limit_bytes=16 * 1024 * 1024),
         name="fill_first",
     )(partner, acquired, rows)
@@ -296,7 +296,7 @@
         in_specs=[smem, smem, smem, smem, vmem, vmem, vmem],
         out_specs=vmem,
         scratch_shapes=[
-            pltpu.VMEM((NB, BS, NS), jnp.bfloat16),
+            pltpu.VMEM((NB, BS, NS), jnp.float32),
             pltpu.VMEM((2 * NS, NS), jnp.bfloat16),
             pltpu.VMEM((2, 2 * OWN, 2 * NS), jnp.bfloat16),
             pltpu.VMEM((2 * OWN, NS), jnp.float32),

time: 91.4 us -> 91.3 us (level)
  no operation moved by 1% of the time
where the time goes in v6:
time: 91.3 us; the launch traced here: 91.1 us
  blocking collectives  61.8 us (68%)
  Pallas kernels  27.9 us (31%)
  waiting for transfers between devices  1.01 us (1%)
    all_to_all x1, blocking collectives, shards(): lax.all_to_all(outgoing, ALL_AXES, split_axis=0, concat_axis=0, tiled=True)  40.8 us
    all_to_all x1, blocking collectives, shards(): lax.all_to_all(estimate, BIN_AXES, split_axis=0, concat_axis=0, tiled=True)  21.1 us
    pallas_call x1, Pallas kernels, solve(): pl.pallas_call(solve_kernel, out_shape=jax.ShapeDtypeStruct((GROUP, 2, BS...  15.1 us
    pallas_call x1, Pallas kernels, transform(): pl.pallas_call(transform_kernel, out_shape=jax.ShapeDtypeStruct((NB, BS,...  5.15 us
    pallas_call x1, Pallas kernels, restore(): pl.pallas_call(restore_kernel, out_shape=jax.ShapeDtypeStruct((BS, NS, NT...  4.43 us
    pallas_call x1, Pallas kernels, fill_first(): pl.pallas_call(fill_first_kernel, out_shape=(jax.ShapeDtypeStruct((NS, NS...  3.17 us
  transfers between devices with their start and end apart: 1, of which 1 were waited for; matrix products, arithmetic and copies ran while one was open for 0% of the time, Pallas kernels for 3%

profile of v6, /device:TPU:0, one launch (start us, length us, event | category | flops | bytes accessed | tf_op | source)
XLA Modules:
  0.0 91.1 jit_solution(9240574774023244330)
XLA Ops:
  0.0 5.2 %transform.1 = bf16[128,8,1024]{2,1,0:T(8,128)(2,1)S(1)} custom-call(bf16[64,512]{1,0:T(8,128)(2,1)} %constant.31.clone.table_from, bf16[8,1024,512]{2,1,0:T(8,128)(2,1)} %traces.1), custom_call_target="tpu_custom_call" | custom-call | tf_op jit(solution)/shard_map/transform/pallas_call | solution.py:64
  5.2 0.0 copy-start.1
  5.2 0.0 copy-start.2
  5.2 40.8 %all_to_all.10.rows = bf16[128,8,1024]{2,1,0:T(8,128)(2,1)S(1)} all-to-all(bf16[128,8,1024]{2,1,0:T(8,128)(2,1)S(1)} %transform.1), channel_id=1, replica_groups=mesh['z_hi'=2,'z_lo'=2,'core'=2,'x'=4,'y'=4] {'z_hi','z_lo','core','x','y'}, dimensions={0} | all-to-all | bytes 4194304 | tf_op jit(solution)/shard_map/all_to_all | solution.py:320
  45.9 0.0 copy-start.3
  45.9 0.0 copy-start.4
  45.9 0.0 collective-permute-start
  46.0 0.1 pad_add_fusion.place
  46.0 0.0 copy-done.1
  46.0 0.0 copy-done.2
  46.0 3.2 %fill_first.1 = (bf16[1024,1024]{1,0:T(8,128)(2,1)S(1)}, f32[128,1024]{1,0:T(8,128)S(1)}) custom-call(s32[128]{0:T(128)S(1)} %copy-done.2, s32[128,128]{1,0:T(8,128)S(1)} %copy-done.1, bf16[128,8,1024]{2,1,0:T(8,128)(2,1)S(1)} %all_to_all.10.rows), custom_call_target="tpu_custom_call" | custom-call | tf_op jit(solution)/shard_map/fill_first/pallas_call | solution.py:180
  49.2 1.0 %collective-permute-done.rows = bf16[128,8,1024]{2,1,0:T(8,128)(2,1)} collective-permute-done((bf16[128,8,1024]{2,1,0:T(8,128)(2,1)S(1)}, bf16[128,8,1024]{2,1,0:T(8,128)(2,1)}, u32[]{:S(2)}, u32[]{:S(2)}) %collective-permute-start) | collective-permute-done | bytes 2097184 | tf_op jit(solution)/shard_map/ppermute | solution.py:321
  50.2 0.0 copy-done.3
  50.2 0.0 copy-done.4
  50.2 15.1 %solve.1 = bf16[32,2,8,1024]{3,2,1,0:T(8,128)(2,1)S(1)} custom-call(s32[128]{0:T(128)S(1)} %copy-done.2, s32[3]{0:T(128)S(1)} %pad_add_fusion.place, s32[8]{0:T(128)S(1)} %copy-done.4, f32[2,8]{1,0:T(2,128)S(1)} %copy-done.3, f32[128,1024]{1,0:T(8,128)S(1)} %get-tuple-element.7.mask, bf16[1024,1024]{1,0:T(8,128)(2,1)S(1)} %get-tuple-element.8.first, ...), custom_call_target="tpu_custom_call" | custom-call | tf_op jit(solution)/shard_map/solve/pallas_call | solution.py:293
  65.4 0.0 copy-start
  65.4 21.1 %all_to_all.11.spectra = bf16[32,2,8,1024]{3,2,1,0:T(8,128)(2,1)S(1)} all-to-all(bf16[32,2,8,1024]{3,2,1,0:T(8,128)(2,1)S(1)} %solve.1), channel_id=1, replica_groups=mesh['z_hi'=2,'z_lo'=2,'core'=2,'x'=4,'y'=4] {'z_lo','x','y'}, dimensions={0} | all-to-all | bytes 2097152 | tf_op jit(solution)/shard_map/all_to_all | solution.py:326
  86.4 0.0 copy-done
  86.4 4.4 %restore.1 = bf16[8,1024,512]{2,1,0:T(8,128)(2,1)} custom-call(s32[3]{0:T(128)S(1)} %pad_add_fusion.place, bf16[32,2,8,1024]{3,2,1,0:T(8,128)(2,1)S(1)} %all_to_all.11.spectra, bf16[2,64,512]{2,1,0:T(8,128)(2,1)S(1)} %copy-done), custom_call_target="tpu_custom_call" | custom-call | tf_op jit(solution)/shard_map/restore/pallas_call | solution.py:101
Async XLA Ops:
  5.2 40.9 %copy-start.1 = (s32[128,128]{1,0:T(8,128)S(1)}, s32[128,128]{1,0:T(8,128)}, u32[]{:S(2)}) copy-start(s32[128,128]{1,0:T(8,128)} %acquired.1) | copy-start | bytes 196612
  5.2 40.9 %copy-start.2 = (s32[128]{0:T(128)S(1)}, s32[128]{0:T(128)}, u32[]{:S(2)}) copy-start(s32[128]{0:T(128)} %partner.3) | copy-start | bytes 1540
  45.9 4.3 %copy-start.3 = (f32[2,8]{1,0:T(2,128)S(1)}, f32[2,8]{1,0:T(2,128)}, u32[]{:S(2)}) copy-start(f32[2,8]{1,0:T(2,128)} %wavelet.1) | copy-start | bytes 196
  45.9 4.3 %copy-start.4 = (s32[8]{0:T(128)S(1)}, s32[8]{0:T(128)}, u32[]{:S(2)}) copy-start(s32[8]{0:T(128)} %band_counts.1) | copy-start | bytes 100
  45.9 4.3 %collective-permute-start = (bf16[128,8,1024]{2,1,0:T(8,128)(2,1)S(1)}, bf16[128,8,1024]{2,1,0:T(8,128)(2,1)}, u32[]{:S(2)}, u32[]{:S(2)}) collective-permute-start(bf16[128,8,1024]{2,1,0:T(8,128)(2,1)S(1)} %all_to_all.10.rows), channel_id=1, source_target_pairs={{0,16},{16,0},{1,17},{17,1},{2,18},{18,2},{3,19},{19,3},{4,20},{20... | collective-permute-start | bytes 6291464 | tf_op jit(solution)/shard_map/ppermute | solution.py:321
  65.4 21.1 %copy-start = (bf16[2,64,512]{2,1,0:T(8,128)(2,1)S(1)}, bf16[2,64,512]{2,1,0:T(8,128)(2,1)}, u32[]{:S(2)}) copy-start(bf16[2,64,512]{2,1,0:T(8,128)(2,1)} %constant.32.clone.tables) | copy-start | bytes 393220

commit v7 on v6

--- a/solution.py
+++ b/solution.py
@@ -160,7 +160,7 @@
     )
 
 
-def fill_first_kernel(partner, acquired, rows, filled, mask, mirror):
+def fill_first_kernel(partner, place, acquired, rows, filled, mask, mine, mirror):
     spread(acquired, mask)
     turn(partner, rows, mirror)
 
@@ -174,21 +174,34 @@
 
     lax.fori_loop(0, NB // 2, pick, 0, unroll=8)
 
-
-def fill_first(partner, acquired, rows):
+    def gather(pair, carry):
+        values = []
+        for i in range(2):
+            member = pair * 2 + i
+            chip = (member % 16) * 4 + member // 16 + place[0]
+            both = filled[pl.ds(pl.multiple_of(chip * 16, 16), 16), :].astype(jnp.float32)
+            values.append(jnp.where(place[1] == 0, both[:BS], both[BS:]))
+        mine[pl.ds(pl.multiple_of(pair * 16, 16), 16), :] = jnp.concatenate(values, axis=0)
+        return carry
+
+    lax.fori_loop(0, GROUP // 2, gather, 0, unroll=4)
+
+
+def fill_first(partner, place, acquired, rows):
     vmem = pl.BlockSpec(memory_space=pltpu.VMEM)
     return pl.pallas_call(
         fill_first_kernel,
         out_shape=(
             jax.ShapeDtypeStruct((NS, NS), jnp.bfloat16),
             jax.ShapeDtypeStruct((NB, NS), jnp.float32),
+            jax.ShapeDtypeStruct((OWN, NS), jnp.float32),
         ),
-        in_specs=[pl.BlockSpec(memory_space=pltpu.SMEM), vmem, vmem],
-        out_specs=(vmem, vmem),
+        in_specs=[pl.BlockSpec(memory_space=pltpu.SMEM)] * 2 + [vmem, vmem],
+        out_specs=(vmem, vmem, vmem),
         scratch_shapes=[pltpu.VMEM((NB, BS, NS), jnp.float32)],
         compiler_params=pltpu.CompilerParams(vmem_limit_bytes=16 * 1024 * 1024),
         name="fill_first",
-    )(partner, acquired, rows)
+    )(partner, place, acquired, rows)
 
 
 def solve_kernel(
@@ -197,6 +210,7 @@
     band_counts,
     wavelet,
     mask,
+    mine,
     first,
     rows,
     out,
@@ -243,20 +257,17 @@
         left[slot, pl.ds(OWN + row, rows), pl.ds(NS + column, columns)] = real_low
 
     def own(pair, carry):
-        reals, imags = [], []
+        imags = []
         for i in range(2):
             member = pair * 2 + i
             chip = (member % 16) * 4 + member // 16 + place[0]
-            both = first[pl.ds(pl.multiple_of(chip * 16, 16), 16), :].astype(jnp.float32)
-            reals.append(jnp.where(place[1] == 0, both[:BS], both[BS:]))
             imags.append(
                 choose(partner, rows, mirror, mask, chip * 2 + place[1], slice(None))
             )
-        real = jnp.concatenate(reals, axis=0)
+        row = pl.multiple_of(pair * 16, 16)
+        real = mine[pl.ds(row, 16), :]
         imag = jnp.concatenate(imags, axis=0)
-        row = pl.multiple_of(pair * 16, 16)
-        base[pl.ds(row, 16), :] = real
-        base[pl.ds(OWN + row, 16), :] = imag
+        base[pl.ds(row, 16), :] = imag
         put(0, row, 16, real, imag, 0, NS)
         return carry
 
@@ -272,38 +283,39 @@
             product = jnp.dot(
                 left[slot], factor[:, columns], preferred_element_type=jnp.float32
             )
-            value = base[:, columns] - product
+            real = mine[:, columns] - product[:OWN]
+            imag = base[:, columns] - product[OWN:]
             if last:
                 out[:, 0, :, columns] = (
-                    value[:OWN].reshape(GROUP, BS, width).astype(jnp.bfloat16)
+                    real.reshape(GROUP, BS, width).astype(jnp.bfloat16)
                 )
                 out[:, 1, :, columns] = (
-                    value[OWN:].reshape(GROUP, BS, width).astype(jnp.bfloat16)
+                    imag.reshape(GROUP, BS, width).astype(jnp.bfloat16)
                 )
             else:
-                put(1 - slot, 0, OWN, value[:OWN], value[OWN:], tile * width, width)
+                put(1 - slot, 0, OWN, real, imag, tile * width, width)
 
     for turn_index in range(ITERS):
         sweep(turn_index % 2, turn_index == 0, turn_index == ITERS - 1)
 
 
-def solve(partner, place, band_counts, wavelet, mask, first, rows):
+def solve(partner, place, band_counts, wavelet, mask, mine, first, rows):
     smem = pl.BlockSpec(memory_space=pltpu.SMEM)
     vmem = pl.BlockSpec(memory_space=pltpu.VMEM)
     return pl.pallas_call(
         solve_kernel,
         out_shape=jax.ShapeDtypeStruct((GROUP, 2, BS, NS), jnp.bfloat16),
-        in_specs=[smem, smem, smem, smem, vmem, vmem, vmem],
+        in_specs=[smem, smem, smem, smem, vmem, vmem, vmem, vmem],
         out_specs=vmem,
         scratch_shapes=[
             pltpu.VMEM((NB, BS, NS), jnp.float32),
             pltpu.VMEM((2 * NS, NS), jnp.bfloat16),
             pltpu.VMEM((2, 2 * OWN, 2 * NS), jnp.bfloat16),
-            pltpu.VMEM((2 * OWN, NS), jnp.float32),
+            pltpu.VMEM((OWN, NS), jnp.float32),
         ],
         compiler_params=pltpu.CompilerParams(vmem_limit_bytes=32 * 1024 * 1024),
         name="solve",
-    )(partner, place, band_counts, wavelet, mask, first, rows)
+    )(partner, place, band_counts, wavelet, mask, mine, first, rows)
 
 
 def shards(recorded, acquired, partner, band_counts, wavelet):
@@ -319,9 +331,9 @@
     )
     first = lax.all_to_all(outgoing, ALL_AXES, split_axis=0, concat_axis=0, tiled=True)
     second = lax.ppermute(first, "core", [(0, 1), (1, 0)])
-    filled, mask = fill_first(partner, acquired, first)
-
-    estimate = solve(partner, place, band_counts, wavelet, mask, filled, second)
+    filled, mask, mine = fill_first(partner, place, acquired, first)
+
+    estimate = solve(partner, place, band_counts, wavelet, mask, mine, filled, second)
 
     returned = lax.all_to_all(estimate, BIN_AXES, split_axis=0, concat_axis=0, tiled=True)
     paired = inverse.reshape(2, NF, NT).transpose(1, 0, 2)

time: 91.3 us -> 91.3 us (level)
  transfers between devices with their start and end apart: 1 -> 1, of which waited for: 1 -> 1; matrix products, arithmetic and copies ran while one was open for 0% -> 0% of each run, Pallas kernels for 3% -> 4%
where the time goes in v7:
time: 91.3 us; the launch traced here: 91.1 us
  blocking collectives  61.8 us (68%)
  Pallas kernels  28.2 us (31%)
    all_to_all x1, blocking collectives, shards(): lax.all_to_all(outgoing, ALL_AXES, split_axis=0, concat_axis=0, tiled=True)  40.8 us
    all_to_all x1, blocking collectives, shards(): lax.all_to_all(estimate, BIN_AXES, split_axis=0, concat_axis=0, tiled=True)  21.1 us
    pallas_call x1, Pallas kernels, solve(): pl.pallas_call(solve_kernel, out_shape=jax.ShapeDtypeStruct((GROUP, 2, BS...  15.2 us
    pallas_call x1, Pallas kernels, transform(): pl.pallas_call(transform_kernel, out_shape=jax.ShapeDtypeStruct((NB, BS,...  5.15 us
    pallas_call x1, Pallas kernels, restore(): pl.pallas_call(restore_kernel, out_shape=jax.ShapeDtypeStruct((BS, NS, NT...  4.43 us
    pallas_call x1, Pallas kernels, fill_first(): pl.pallas_call(fill_first_kernel, out_shape=(jax.ShapeDtypeStruct((NS, NS...  3.5 us
  transfers between devices with their start and end apart: 1, of which 1 were waited for; matrix products, arithmetic and copies ran while one was open for 0% of the time, Pallas kernels for 4%

profile of v7, /device:TPU:0, one launch (start us, length us, event | category | flops | bytes accessed | tf_op | source)
XLA Modules:
  0.0 91.1 jit_solution(654205242752694008)
XLA Ops:
  0.0 5.2 %transform.1 = bf16[128,8,1024]{2,1,0:T(8,128)(2,1)S(1)} custom-call(bf16[64,512]{1,0:T(8,128)(2,1)} %constant.31.clone.table_from, bf16[8,1024,512]{2,1,0:T(8,128)(2,1)} %traces.1), custom_call_target="tpu_custom_call" | custom-call | tf_op jit(solution)/shard_map/transform/pallas_call | solution.py:64
  5.2 0.0 copy-start.1
  5.2 0.0 copy-start.2
  5.2 40.8 %all_to_all.10.rows = bf16[128,8,1024]{2,1,0:T(8,128)(2,1)S(1)} all-to-all(bf16[128,8,1024]{2,1,0:T(8,128)(2,1)S(1)} %transform.1), channel_id=1, replica_groups=mesh['z_hi'=2,'z_lo'=2,'core'=2,'x'=4,'y'=4] {'z_hi','z_lo','core','x','y'}, dimensions={0} | all-to-all | bytes 4194304 | tf_op jit(solution)/shard_map/all_to_all | solution.py:332
  45.9 0.0 copy-start.3
  45.9 0.0 copy-start.4
  45.9 0.0 collective-permute-start
  46.0 0.1 pad_add_fusion.place
  46.0 0.0 copy-done.1
  46.0 0.0 copy-done.2
  46.0 3.5 %fill_first.1 = (bf16[1024,1024]{1,0:T(8,128)(2,1)S(1)}, f32[128,1024]{1,0:T(8,128)S(1)}, f32[256,1024]{1,0:T(8,128)S(1)}) custom-call(s32[128]{0:T(128)S(1)} %copy-done.2, s32[3]{0:T(128)S(1)} %pad_add_fusion.place, s32[128,128]{1,0:T(8,128)S(1)} %copy-done.1, bf16[128,8,1024]{2,1,0:T(8,128)(2,1)S(1)} %all_to_all.10.rows), custom_call_target="tpu_custom_call" | custom-call | tf_op jit(solution)/shard_map/fill_first/pallas_call | solution.py:192
  49.5 0.7 collective-permute-done.rows
  50.2 0.0 copy-done.3
  50.2 0.0 copy-done.4
  50.2 15.2 %solve.1 = bf16[32,2,8,1024]{3,2,1,0:T(8,128)(2,1)S(1)} custom-call(s32[128]{0:T(128)S(1)} %copy-done.2, s32[3]{0:T(128)S(1)} %pad_add_fusion.place, s32[8]{0:T(128)S(1)} %copy-done.4, f32[2,8]{1,0:T(2,128)S(1)} %copy-done.3, f32[128,1024]{1,0:T(8,128)S(1)} %get-tuple-element.8.mask, f32[256,1024]{1,0:T(8,128)S(1)} %get-tuple-element.9.mine, ...), custom_call_target="tpu_custom_call" | custom-call | tf_op jit(solution)/shard_map/solve/pallas_call | solution.py:305
  65.4 0.0 copy-start
  65.4 21.1 %all_to_all.11.spectra = bf16[32,2,8,1024]{3,2,1,0:T(8,128)(2,1)S(1)} all-to-all(bf16[32,2,8,1024]{3,2,1,0:T(8,128)(2,1)S(1)} %solve.1), channel_id=1, replica_groups=mesh['z_hi'=2,'z_lo'=2,'core'=2,'x'=4,'y'=4] {'z_lo','x','y'}, dimensions={0} | all-to-all | bytes 2097152 | tf_op jit(solution)/shard_map/all_to_all | solution.py:338
  86.5 0.0 copy-done
  86.5 4.4 %restore.1 = bf16[8,1024,512]{2,1,0:T(8,128)(2,1)} custom-call(s32[3]{0:T(128)S(1)} %pad_add_fusion.place, bf16[32,2,8,1024]{3,2,1,0:T(8,128)(2,1)S(1)} %all_to_all.11.spectra, bf16[2,64,512]{2,1,0:T(8,128)(2,1)S(1)} %copy-done), custom_call_target="tpu_custom_call" | custom-call | tf_op jit(solution)/shard_map/restore/pallas_call | solution.py:101
Async XLA Ops:
  5.2 40.9 %copy-start.1 = (s32[128,128]{1,0:T(8,128)S(1)}, s32[128,128]{1,0:T(8,128)}, u32[]{:S(2)}) copy-start(s32[128,128]{1,0:T(8,128)} %acquired.1) | copy-start | bytes 196612
  5.2 40.9 %copy-start.2 = (s32[128]{0:T(128)S(1)}, s32[128]{0:T(128)}, u32[]{:S(2)}) copy-start(s32[128]{0:T(128)} %partner.3) | copy-start | bytes 1540
  45.9 4.3 %copy-start.3 = (f32[2,8]{1,0:T(2,128)S(1)}, f32[2,8]{1,0:T(2,128)}, u32[]{:S(2)}) copy-start(f32[2,8]{1,0:T(2,128)} %wavelet.1) | copy-start | bytes 196
  45.9 4.3 %copy-start.4 = (s32[8]{0:T(128)S(1)}, s32[8]{0:T(128)}, u32[]{:S(2)}) copy-start(s32[8]{0:T(128)} %band_counts.1) | copy-start | bytes 100
  45.9 4.3 %collective-permute-start = (bf16[128,8,1024]{2,1,0:T(8,128)(2,1)S(1)}, bf16[128,8,1024]{2,1,0:T(8,128)(2,1)}, u32[]{:S(2)}, u32[]{:S(2)}) collective-permute-start(bf16[128,8,1024]{2,1,0:T(8,128)(2,1)S(1)} %all_to_all.10.rows), channel_id=1, source_target_pairs={{0,16},{16,0},{1,17},{17,1},{2,18},{18,2},{3,19},{19,3},{4,20},{20... | collective-permute-start | bytes 6291464 | tf_op jit(solution)/shard_map/ppermute | solution.py:333
  65.4 21.1 %copy-start = (bf16[2,64,512]{2,1,0:T(8,128)(2,1)S(1)}, bf16[2,64,512]{2,1,0:T(8,128)(2,1)}, u32[]{:S(2)}) copy-start(bf16[2,64,512]{2,1,0:T(8,128)(2,1)} %constant.32.clone.tables) | copy-start | bytes 393220
